TPU v7x, 32 devices: a whole 2x2x4 slice. The times are simulated.
32 devices in a mesh: grp: 2 (over y), ctx: 16 (over z, x, core).
Axes of the slice: x: 2, y: 2, z: 4, core: 2. Of those that a mesh axis runs over, the one named last changes fastest.
Arguments:
- query_rows: bfloat16 [4096, 4096], P(('grp', 'ctx')), parts along dimension 0, may hold values from -6 to 6
- key_rows: bfloat16 [4096, 4096], P(('grp', 'ctx')), parts along dimension 0, may hold values from -6 to 6
- value_rows: bfloat16 [4096, 4096], P(('grp', 'ctx')), parts along dimension 0, may hold values from -6 to 6
- grad_out: bfloat16 [4096, 4096], P(('grp', 'ctx')), parts along dimension 0, may hold values from -6 to 6
- conv_filter: bfloat16 [256, 128], replicated, may hold values from -0.44194174 to 0.44194174
Outputs:
- grad_query: bfloat16 [4096, 4096], P(('grp', 'ctx')), parts along dimension 0
- grad_key: bfloat16 [4096, 4096], P(('grp', 'ctx')), parts along dimension 0
- grad_value: bfloat16 [4096, 4096], P(('grp', 'ctx')), parts along dimension 0
- grad_filter: float32 [512, 128], P(('grp', 'ctx')), parts along dimension 0
There are 2 independent parts, one for each index of `grp`. A program takes and returns all parts, laid end to end along the dimension named above; an argument that names none is the same for every part. Nothing has to cross between parts.
All inputs are finite; a program needn't handle non-finite values.
Results may differ from a plain program's by a relative error of at most 0.005.
Values may be sent and summed in bfloat16 or wider, within the bound.
No kernel may reach another device: no remote copies, remote signals or barrier semaphores. Data moves between devices by JAX's collectives and lax.ppermute only.
A program may use at most 64 MiB of HBM per device.

v0:
```python
import math

import jax
import jax.numpy as jnp
from jax import lax
from jax.sharding import PartitionSpec as P

GSIZE = 16
TAPS = 128


def toeplitz(filter_rows, offsets):
    taps_index = lax.broadcasted_iota(jnp.int32, offsets.shape + (TAPS,), 2)
    selector = (offsets[:, :, None] == taps_index).astype(filter_rows.dtype)
    picked = jnp.einsum("gj,tsj->gts", filter_rows, selector, preferred_element_type=jnp.float32)
    return picked.astype(filter_rows.dtype)


def block_terms(prod_now, prod_before, grad_now, grad_after, filter_rows):
    block_total, block_rows, channels = prod_now.shape
    rim_rows = prod_before.shape[1]
    groups_here = channels // GSIZE
    row_index = lax.broadcasted_iota(jnp.int32, (block_rows, block_rows + rim_rows), 0)
    col_index = lax.broadcasted_iota(jnp.int32, (block_rows, block_rows + rim_rows), 1)
    causal = toeplitz(filter_rows, rim_rows + row_index - col_index)
    future = toeplitz(filter_rows, col_index - row_index)
    extended = jnp.concatenate([prod_before, prod_now], axis=1).reshape(
        block_total, block_rows + rim_rows, groups_here, GSIZE
    )
    grads_ahead = jnp.concatenate([grad_now, grad_after], axis=1).reshape(
        block_total, block_rows + rim_rows, groups_here, GSIZE
    )
    mixed_sum = jnp.einsum("gts,bsgc->btgc", causal, extended, preferred_element_type=jnp.float32)
    back_sum = jnp.einsum("gts,bsgc->btgc", future, grads_ahead, preferred_element_type=jnp.float32)
    grads_here = grad_now.reshape(block_total, block_rows, groups_here, GSIZE)
    pair_sums = jnp.einsum(
        "btgc,bsgc->gts", grads_here, extended, preferred_element_type=jnp.float32
    )
    flattened = pair_sums.reshape(groups_here, block_rows * (block_rows + rim_rows))
    flattened = jnp.pad(flattened, ((0, 0), (0, block_rows)))
    skewed = flattened.reshape(groups_here, block_rows, block_rows + rim_rows + 1)
    picked = skewed[:, :, rim_rows - TAPS + 1 : rim_rows + 1]
    filter_part = jnp.flip(jnp.sum(picked, axis=1), axis=1)
    shape_out = (block_total, block_rows, channels)
    return (mixed_sum.reshape(shape_out), back_sum.reshape(shape_out), filter_part)


def window_terms(prod_now, prod_before, grad_now, grad_after, filter_rows, sub_rows):
    block_total, block_rows, channels = prod_now.shape
    sub_count = block_rows // sub_rows
    prod_full = jnp.concatenate([prod_before, prod_now], axis=1)
    prod_full = prod_full.reshape(block_total, (block_rows + TAPS) // sub_rows, sub_rows, channels)
    grad_full = jnp.concatenate([grad_now, grad_after], axis=1)
    grad_full = grad_full.reshape(block_total, (block_rows + TAPS) // sub_rows, sub_rows, channels)
    before_win = prod_full[:, 0:sub_count]
    after_win = grad_full[:, 1 : 1 + sub_count]
    flat_count = block_total * sub_count
    mixed_sum, back_sum, filter_part = block_terms(
        prod_now,
        before_win.reshape(flat_count, TAPS, channels),
        grad_now,
        after_win.reshape(flat_count, TAPS, channels),
        filter_rows,
    )
    return (mixed_sum, back_sum, filter_part)


def run_blocks(prod_now, prod_before, grad_now, grad_after, filter_rows, sub_rows):
    block_total, block_rows, channels = prod_now.shape
    block_width = min(512, channels)
    block_count = channels // block_width

    def to_blocks(array):
        return jnp.moveaxis(
            array.reshape(array.shape[0], array.shape[1], block_count, block_width), 2, 0
        )

    def from_blocks(array):
        return jnp.moveaxis(array, 0, 2).reshape(block_total, block_rows, channels)

    def one_block(block_items):
        return window_terms(
            block_items[0], block_items[1], block_items[2], block_items[3], block_items[4], sub_rows
        )

    block_items = (
        to_blocks(prod_now),
        to_blocks(prod_before),
        to_blocks(grad_now),
        to_blocks(grad_after),
        filter_rows.reshape(block_count, block_width // GSIZE, TAPS),
    )
    mixed_sum, back_sum, filter_part = lax.map(one_block, block_items)
    return (
        from_blocks(mixed_sum),
        from_blocks(back_sum),
        filter_part.reshape(channels // GSIZE, TAPS),
    )


def shards(query_rows, key_rows, value_rows, grad_out, conv_filter):
    product = (key_rows.astype(jnp.float32) * value_rows.astype(jnp.float32)).astype(jnp.bfloat16)
    gated_grad = (grad_out.astype(jnp.float32) * query_rows.astype(jnp.float32)).astype(
        jnp.bfloat16
    )
    local_rows = product.shape[0]
    moved_prod, moved_grad = (
        lax.all_to_all(product, "ctx", split_axis=1, concat_axis=0, tiled=True),
        lax.all_to_all(gated_grad, "ctx", split_axis=1, concat_axis=0, tiled=True),
    )
    total_rows, channels = moved_prod.shape
    block_total = total_rows // TAPS
    blocks_prod = moved_prod.reshape(block_total, TAPS, channels)
    blocks_grad = moved_grad.reshape(block_total, TAPS, channels)
    zero_block = jnp.zeros((1, TAPS, channels), jnp.bfloat16)
    rows_before = jnp.concatenate([zero_block, blocks_prod[:-1]], axis=0)
    rows_after = jnp.concatenate([blocks_grad[1:], zero_block], axis=0)
    groups_here = channels // GSIZE
    own_filter = lax.dynamic_slice_in_dim(
        conv_filter, lax.axis_index("ctx") * groups_here, groups_here, 0
    )
    mixed_sum, back_sum, filter_part = run_blocks(
        blocks_prod, rows_before, blocks_grad, rows_after, own_filter, TAPS
    )
    mixed_sum = mixed_sum.reshape(total_rows, channels)
    back_sum = back_sum.reshape(total_rows, channels)
    mixed_home, back_home = (
        lax.all_to_all(mixed_sum, "ctx", split_axis=0, concat_axis=1, tiled=True),
        lax.all_to_all(back_sum, "ctx", split_axis=0, concat_axis=1, tiled=True),
    )
    grad_scale = 1.0 / math.sqrt(local_rows * lax.axis_size("ctx") * GSIZE)
    grad_query = (grad_out.astype(jnp.float32) * mixed_home).astype(jnp.bfloat16)
    grad_key = (back_home * value_rows.astype(jnp.float32)).astype(jnp.bfloat16)
    grad_value = (back_home * key_rows.astype(jnp.float32)).astype(jnp.bfloat16)
    return (grad_query, grad_key, grad_value, filter_part * grad_scale)


def solution(mesh):
    return jax.shard_map(
        shards,
        mesh=mesh,
        in_specs=(
            P(("grp", "ctx"), None),
            P(("grp", "ctx"), None),
            P(("grp", "ctx"), None),
            P(("grp", "ctx"), None),
            P(),
        ),
        out_specs=(
            P(("grp", "ctx"), None),
            P(("grp", "ctx"), None),
            P(("grp", "ctx"), None),
            P(("grp", "ctx"), None),
        ),
        check_vma=False,
    )
```

profile of v0, /device:TPU:15, one launch (start us, length us, event | category | flops | bytes accessed | tf_op | source)
XLA Modules:
  0.0 199.6 jit_solution(10627907065178947283)
XLA Ops:
  0.6 1.8 fusion.7
  2.5 1.3 copy.47
  3.8 6.5 %all-to-all-start.2 = ((bf16[128,16,256]{0,2,1:T(8,128)(2,1)}), bf16[128,16,256]{0,2,1:T(8,128)(2,1)S(1)}, u32[]{:S(2)}, u32[]{:S(2)}) async-start(bf16[128,16,256]{0,2,1:T(8,128)(2,1)} %bitcast.11), calls=%async_computation.2 | async-start | bytes 2097152 | tf_op jit(solution)/shard_map/all_to_all | solution.py:109
  10.3 8.2 %fusion.26 = bf16[16,128,256,1]{2,0,1,3:T(8,128)(2,1)} fusion(s32[128,256]{1,0:T(8,128)S(1)} %iota_subtract_fusion, bf16[256,128]{1,0:T(8,128)(2,1)S(1)} %copy-done, s32[]{:T(128)S(6)} %select_n.3), kind=kOutput, calls=%fused_computation.33 | convolution fusion | flops 138936320 | bytes 1183748 | tf_op jit(solution)/shard_map/while/body/eval_jaxpr/gj,tsj->gts/dot_general | solution.py:15
  18.5 16.7 %all-to-all-done.2 = bf16[128,16,256]{0,2,1:T(8,128)(2,1)S(1)} async-done(((bf16[128,16,256]{0,2,1:T(8,128)(2,1)}), bf16[128,16,256]{0,2,1:T(8,128)(2,1)S(1)}, u32[]{:S(2)}, u32[]{:S(2)}) %all-to-all-start.2) | async-done | bytes 1048608 | tf_op jit(solution)/shard_map/all_to_all | solution.py:109
  35.5 2.1 %reshape.111 = bf16[16,2,128,256]{2,1,3,0:T(2,128)(2,1)} reshape(bf16[16,256,256]{1,2,0:T(8,128)(2,1)S(1)} %fusion.11) | data formatting | bytes 4194304 | tf_op jit(solution)/shard_map/while/body/eval_jaxpr/reshape | solution.py:54
  37.6 4.0 %slice.28 = bf16[16,1,128,256]{2,1,3,0:T(2,128)(2,1)S(1)} slice(bf16[16,2,128,256]{2,1,3,0:T(2,128)(2,1)} %reshape.111), slice={[0:16], [1:2], [0:128], [0:256]} | slice | bytes 2097152 | tf_op jit(solution)/shard_map/while/body/eval_jaxpr/slice | solution.py:56
  43.5 1.6 copy.52
  45.1 4.8 %all-to-all-start.3 = ((f32[16,128,256]{1,2,0:T(8,128)}), f32[16,128,256]{1,2,0:T(8,128)S(1)}, u32[]{:S(2)}, u32[]{:S(2)}) async-start(f32[16,128,256]{1,2,0:T(8,128)} %bitcast.49), calls=%async_computation.3 | async-start | bytes 4194304 | tf_op jit(solution)/shard_map/all_to_all | solution.py:129
  49.9 2.3 %copy.38 = bf16[128,4096]{0,1:T(8,128)(2,1)} copy(bf16[128,4096]{1,0:T(8,128)(2,1)} %param.6) | data formatting | bytes 2097152 | tf_op args[1]
  52.2 2.3 %copy.39 = bf16[128,4096]{0,1:T(8,128)(2,1)} copy(bf16[128,4096]{1,0:T(8,128)(2,1)} %param.7) | data formatting | bytes 2097152 | tf_op args[2]
  54.5 42.9 %all-to-all-done.3 = f32[16,128,256]{1,2,0:T(8,128)S(1)} async-done(((f32[16,128,256]{1,2,0:T(8,128)}), f32[16,128,256]{1,2,0:T(8,128)S(1)}, u32[]{:S(2)}, u32[]{:S(2)}) %all-to-all-start.3) | async-done | bytes 2097184 | tf_op jit(solution)/shard_map/all_to_all | solution.py:129
  97.4 3.6 %fusion.8 = (bf16[128,4096]{0,1:T(8,128)(2,1)}, bf16[128,4096]{0,1:T(8,128)(2,1)}, bf16[128,4096]{0,1:T(8,128)(2,1)}) fusion(bf16[128,4096]{0,1:T(8,128)(2,1)} %copy.38, f32[16,128,256]{1,2,0:T(8,128)S(1)} %all-to-all-done.3, bf16[128,4096]{0,1:T(8,128)(2,1)} %copy.39), kind=kLoop, calls=%fused_computation.17 | loop fusion | flops 4194304 | bytes 7340032 | tf_op jit(solution)/shard_map/convert_element_type | solution.py:134
  100.9 4.8 %all-to-all-start = ((bf16[128,16,256]{0,2,1:T(8,128)(2,1)}), bf16[128,16,256]{0,2,1:T(8,128)(2,1)S(1)}, u32[]{:S(2)}, u32[]{:S(2)}) async-start(bf16[128,16,256]{0,2,1:T(8,128)(2,1)} %bitcast.55), calls=%async_computation | async-start | bytes 2097152 | tf_op jit(solution)/shard_map/all_to_all | solution.py:108
  105.8 8.2 %fusion.25 = bf16[16,128,256,1]{2,0,1,3:T(8,128)(2,1)} fusion(s32[128,256]{1,0:T(8,128)S(1)} %iota_subtract_fusion.1, bf16[256,128]{1,0:T(8,128)(2,1)S(1)} %copy-done, s32[]{:T(128)S(6)} %select_n.3), kind=kOutput, calls=%fused_computation.32 | convolution fusion | flops 138936320 | bytes 1183748 | tf_op jit(solution)/shard_map/while/body/eval_jaxpr/gj,tsj->gts/dot_general | solution.py:15
  114.0 16.6 %all-to-all-done = bf16[128,16,256]{0,2,1:T(8,128)(2,1)S(1)} async-done(((bf16[128,16,256]{0,2,1:T(8,128)(2,1)}), bf16[128,16,256]{0,2,1:T(8,128)(2,1)S(1)}, u32[]{:S(2)}, u32[]{:S(2)}) %all-to-all-start) | async-done | bytes 1048608 | tf_op jit(solution)/shard_map/all_to_all | solution.py:108
  130.7 1.6 fusion.12
  132.2 3.9 %copy.40 = bf16[16,256,256]{2,1,0:T(8,128)(2,1)} copy(bf16[16,256,256]{1,2,0:T(8,128)(2,1)} %fusion.12) | data formatting | bytes 4194304 | tf_op jit(solution)/shard_map/while/body/eval_jaxpr/concatenate | solution.py:51
  136.2 2.3 %slice.26 = bf16[16,1,128,256]{3,2,1,0:T(8,128)(2,1)} slice(bf16[16,2,128,256]{3,2,1,0:T(8,128)(2,1)} %bitcast.52), slice={[0:16], [0:1], [0:128], [0:256]} | slice | bytes 2097152 | tf_op jit(solution)/shard_map/while/body/eval_jaxpr/slice | solution.py:55
  138.5 1.6 copy.41
  140.1 2.3 %fusion.17 = f32[16,128,16,16]{1,3,0,2:T(8,128)S(1)} fusion(bf16[16,128,256,1]{2,0,1,3:T(8,128)(2,1)} %fusion.25, bf16[16,128,16,16]{1,3,2,0:T(8,128)(2,1)S(1)} %bitcast.46, bf16[16,128,16,16]{1,3,2,0:T(8,128)(2,1)S(1)} %bitcast.53), kind=kOutput, calls=%fused_computation.28 | convolution fusion | flops 272629760 | bytes 5242880 | tf_op jit(solution)/shard_map/while/body/eval_jaxpr/gts,bsgc->btgc/dot_general | solution.py:33
  142.4 1.6 copy.45
  144.0 4.8 %all-to-all-start.1 = ((f32[16,128,256]{1,2,0:T(8,128)}), f32[16,128,256]{1,2,0:T(8,128)}, u32[]{:S(2)}, u32[]{:S(2)}) async-start(f32[16,128,256]{1,2,0:T(8,128)} %bitcast.48), calls=%async_computation.1 | async-start | bytes 4194304 | tf_op jit(solution)/shard_map/all_to_all | solution.py:128
  148.8 2.4 %copy.55 = bf16[128,4096]{1,0:T(8,128)(2,1)} copy(bf16[128,4096]{0,1:T(8,128)(2,1)} %get-tuple-element.26) | data formatting | bytes 2097152
  151.2 1.3 copy.54
  152.5 1.7 fusion.35
  154.2 1.2 copy.65
  155.6 3.6 %reshape.113 = f32[16,128,257]{2,1,0:T(8,128)} reshape(f32[16,32896]{1,0:T(8,128)S(1)} %pad.7) | data formatting | bytes 4210688 | tf_op jit(solution)/shard_map/while/body/eval_jaxpr/reshape | solution.py:41
  159.3 1.9 slice_reduce_fusion
  161.9 34.5 %all-to-all-done.1 = f32[16,128,256]{1,2,0:T(8,128)} async-done(((f32[16,128,256]{1,2,0:T(8,128)}), f32[16,128,256]{1,2,0:T(8,128)}, u32[]{:S(2)}, u32[]{:S(2)}) %all-to-all-start.1) | async-done | bytes 2097184 | tf_op jit(solution)/shard_map/all_to_all | solution.py:128
  196.4 2.0 %copy.46 = f32[128,4096]{1,0:T(8,128)S(1)} copy(f32[128,4096]{0,1:T(8,128)} %bitcast.10) | data formatting | bytes 4194304 | tf_op jit(solution)/shard_map/all_to_all | solution.py:128
  198.4 1.2 fusion.6
  (21 shorter events, 3.3 us)
Async XLA Ops:
  0.6 9.7 %copy-start = (bf16[256,128]{1,0:T(8,128)(2,1)S(1)}, bf16[256,128]{1,0:T(8,128)(2,1)}, u32[]{:S(2)}) copy-start(bf16[256,128]{1,0:T(8,128)(2,1)} %param.9) | copy-start | bytes 196612
  3.8 31.4 %all-to-all-start.2 = ((bf16[128,16,256]{0,2,1:T(8,128)(2,1)}), bf16[128,16,256]{0,2,1:T(8,128)(2,1)S(1)}, u32[]{:S(2)}, u32[]{:S(2)}) async-start(bf16[128,16,256]{0,2,1:T(8,128)(2,1)} %bitcast.11), calls=%async_computation.2 | async-start | bytes 2097152 | tf_op jit(solution)/shard_map/all_to_all | solution.py:109
  41.6 1.2 copy-start.4
  45.1 52.2 %all-to-all-start.3 = ((f32[16,128,256]{1,2,0:T(8,128)}), f32[16,128,256]{1,2,0:T(8,128)S(1)}, u32[]{:S(2)}, u32[]{:S(2)}) async-start(f32[16,128,256]{1,2,0:T(8,128)} %bitcast.49), calls=%async_computation.3 | async-start | bytes 4194304 | tf_op jit(solution)/shard_map/all_to_all | solution.py:129
  100.9 29.6 %all-to-all-start = ((bf16[128,16,256]{0,2,1:T(8,128)(2,1)}), bf16[128,16,256]{0,2,1:T(8,128)(2,1)S(1)}, u32[]{:S(2)}, u32[]{:S(2)}) async-start(bf16[128,16,256]{0,2,1:T(8,128)(2,1)} %bitcast.55), calls=%async_computation | async-start | bytes 2097152 | tf_op jit(solution)/shard_map/all_to_all | solution.py:108
  140.1 2.3 %copy-start.2 = (bf16[16,1,128,256]{2,3,0,1:T(8,128)(2,1)}, bf16[16,1,128,256]{2,3,0,1:T(8,128)(2,1)S(1)}, u32[]{:S(2)}) copy-start(bf16[16,1,128,256]{2,3,0,1:T(8,128)(2,1)S(1)} %copy.41) | copy-start | bytes 3145732
  144.0 52.4 %all-to-all-start.1 = ((f32[16,128,256]{1,2,0:T(8,128)}), f32[16,128,256]{1,2,0:T(8,128)}, u32[]{:S(2)}, u32[]{:S(2)}) async-start(f32[16,128,256]{1,2,0:T(8,128)} %bitcast.48), calls=%async_computation.1 | async-start | bytes 4194304 | tf_op jit(solution)/shard_map/all_to_all | solution.py:128
  148.8 2.4 %copy-start.1 = (bf16[128,4096]{0,1:T(8,128)(2,1)S(1)}, bf16[128,4096]{0,1:T(8,128)(2,1)}, u32[]{:S(2)}) copy-start(bf16[128,4096]{0,1:T(8,128)(2,1)} %get-tuple-element.36) | copy-start | bytes 3145732
  196.4 2.0 %copy-start.3 = (bf16[128,4096]{1,0:T(8,128)(2,1)S(1)}, bf16[128,4096]{1,0:T(8,128)(2,1)}, u32[]{:S(2)}) copy-start(bf16[128,4096]{1,0:T(8,128)(2,1)} %param.8) | copy-start | bytes 3145732
where the time goes:
time: 200 us
  waiting for transfers between devices  111 us (56%)
  local copies, waits for them, and re-layouts  35 us (18%)
  matrix products  21.1 us (11%)
  starting transfers between devices  21 us (10%)
  other arithmetic  11.1 us (6%)
    all_to_all x1, waiting for transfers between devices, shards(): lax.all_to_all(back_sum, 'ctx', split_axis=0, concat_axis=1, tiled=True)  42.9 us
    all_to_all x1, waiting for transfers between devices, shards(): lax.all_to_all(mixed_sum, 'ctx', split_axis=0, concat_axis=1, tiled=True)  34.5 us
    all_to_all x1, waiting for transfers between devices, shards(): lax.all_to_all(gated_grad, 'ctx', split_axis=1, concat_axis=0, tiled=True)  16.7 us
    all_to_all x1, waiting for transfers between devices, shards(): lax.all_to_all(product, 'ctx', split_axis=1, concat_axis=0, tiled=True)  16.6 us
    dot_general x2, matrix products, toeplitz(): jnp.einsum('gj,tsj->gts', filter_rows, selector, preferred_element_type=j...  16.3 us
    unnamed x16, local copies, waits for them, and re-layouts  10.6 us
    all_to_all x1, starting transfers between devices, shards(): lax.all_to_all(gated_grad, 'ctx', split_axis=1, concat_axis=0, tiled=True)  6.52 us
    all_to_all x1, starting transfers between devices, shards(): lax.all_to_all(back_sum, 'ctx', split_axis=0, concat_axis=1, tiled=True)  4.83 us
  transfers between devices with their start and end apart: 4, of which 4 were waited for; matrix products, arithmetic and copies ran while one was open for 17% of the time, Pallas kernels for 0%

commit v1 on v0

v1 whole, which is shorter than its diff:
```python
import math

import jax
import jax.numpy as jnp
from jax import lax
from jax.experimental import pallas as pl
from jax.experimental.pallas import tpu as pltpu
from jax.sharding import PartitionSpec as P

GSIZE = 16
B=16; LN=128; NB=8
f32=jnp.float32; bf=jnp.bfloat16
def lanes(shape): return lax.broadcasted_iota(jnp.int32, shape, 1)
def subl(shape): return lax.broadcasted_iota(jnp.int32, shape, 0)
def network(vs):
    shape=vs[0].shape
    lane=lanes(shape)
    cur=[vs[(-m)%NB] for m in range(NB)]
    for bit in (1,2,4):
        mask=(lane & (bit*16))!=0
        cur=[jnp.where(mask,cur[(m-bit)%NB],cur[m]) for m in range(NB)]
    return cur
def rot(x,s):
    s%=LN
    return x if s==0 else pltpu.roll(x,s,1)
def to_groups(tile):
    return network([rot(tile[B*a:B*a+B,:],16*a) for a in range(NB)])
def to_tokens(vs):
    es=network(vs)
    return [rot(e,-16*a) for a,e in enumerate(es)]
def unfold_back(now,bef,g):
    lane=lanes(now.shape)
    blk=((lane>>4)-g)&7
    out=[]
    for e in range(9):
        d=8-e
        if d==8: out.append(bef)
        elif d==0: out.append(now)
        else: out.append(rot(jnp.where(blk<8-d,now,bef),16*d))
    return jnp.concatenate(out,0)
def unfold_fwd(now,aft,g):
    lane=lanes(now.shape)
    blk=((lane>>4)-g)&7
    out=[]
    for d in range(9):
        if d==0: out.append(now)
        elif d==8: out.append(aft)
        else: out.append(rot(jnp.where(blk>=d,now,aft),-16*d))
    return jnp.concatenate(out,0)

def prep_kernel(h_ref,hr_ref,p_ref,g_ref,tm_ref,tb_ref,pn_ref,gn_ref,gr_ref):
    nt=p_ref.shape[1]//LN
    lane=lanes((B,LN)); row=subl((B,LN))
    def body(j,_):
        off=pl.multiple_of(j*LN,LN)
        for src,dst in ((p_ref,pn_ref),(g_ref,gn_ref)):
            tile=src[:,pl.ds(off,LN)]
            for gi,x in enumerate(to_groups(tile)):
                dst[pl.ds(pl.multiple_of((j*NB+gi)*B,B),B),:]=x
        flip=jnp.where(lanes((B,B))+subl((B,B))==B-1,1.,0.).astype(bf)
        for gi in range(NB):
            r0=pl.ds(pl.multiple_of((j*NB+gi)*B,B),B)
            gr_ref[r0,:]=jnp.dot(flip,gn_ref[r0,:],preferred_element_type=f32).astype(bf)
        hs=h_ref[pl.ds(pl.multiple_of(j*NB,NB),NB),:]
        hrs=hr_ref[pl.ds(pl.multiple_of(j*NB,NB),NB),:]
        for gi in range(NB):
            r0=pl.ds(pl.multiple_of((j*NB+gi)*B,B),B)
            rm=pltpu.roll(jnp.broadcast_to(hrs[gi:gi+1,:],(B,LN)),1,1,stride=1,stride_axis=0)
            tm_ref[r0,0:LN]=jnp.where(lane>row,rm,0.).astype(bf)
            tm_ref[r0,LN:2*LN]=jnp.where(lane<=row,rm,0.).astype(bf)
            rb=pltpu.roll(jnp.broadcast_to(hs[gi:gi+1,:],(B,LN)),0,1,stride=1,stride_axis=0)
            tb_ref[r0,0:LN]=jnp.where(lane>=row,rb,0.).astype(bf)
            tb_ref[r0,LN:2*LN]=jnp.where(lane<row,rb,0.).astype(bf)
        return 0
    lax.fori_loop(0,nt,body,0)

def mixed_kernel(tm_ref,pn_ref,gr_ref,bef_ref,go_ref,gq_ref,f_ref):
    nt=bef_ref.shape[1]//LN
    lane=lanes((B,LN)); row=subl((B,LN))
    def body(j,_):
        off=pl.multiple_of(j*LN,LN)
        bef=to_groups(bef_ref[:,pl.ds(off,LN)])
        ys=[];fr=[]
        for gi in range(NB):
            r0=pl.ds(pl.multiple_of((j*NB+gi)*B,B),B)
            xu=unfold_back(pn_ref[r0,:],bef[gi],gi)
            ys.append(jnp.dot(tm_ref[r0,0:9*B],xu,preferred_element_type=f32))
            F=lax.dot_general(gr_ref[r0,:],xu,(((1,),(1,)),((),())),preferred_element_type=f32)
            F2=jnp.concatenate([F[:,LN:LN+B],jnp.zeros((B,LN-B),f32)],1)
            C=jnp.where(lane+row<=B-1,F2,F[:,:LN])
            fr.append(jnp.sum(pltpu.roll(C,LN-B,1,stride=1,stride_axis=0),0,keepdims=True))
        f_ref[pl.ds(pl.multiple_of(j*NB,NB),NB),:]=jnp.concatenate(fr,0)
        for a,y in enumerate(to_tokens(ys)):
            go=go_ref[B*a:B*a+B,pl.ds(off,LN)].astype(f32)
            gq_ref[B*a:B*a+B,pl.ds(off,LN)]=(go*y).astype(bf)
        return 0
    lax.fori_loop(0,nt,body,0)

def back_kernel(tb_ref,gn_ref,aft_ref,k_ref,v_ref,gk_ref,gv_ref):
    nt=aft_ref.shape[1]//LN
    def body(j,_):
        off=pl.multiple_of(j*LN,LN)
        aft=to_groups(aft_ref[:,pl.ds(off,LN)])
        ys=[]
        for gi in range(NB):
            r0=pl.ds(pl.multiple_of((j*NB+gi)*B,B),B)
            xu=unfold_fwd(gn_ref[r0,:],aft[gi],gi)
            ys.append(jnp.dot(tb_ref[r0,0:9*B],xu,preferred_element_type=f32))
        for a,y in enumerate(to_tokens(ys)):
            sl=(slice(B*a,B*a+B),pl.ds(off,LN))
            gk_ref[sl]=(v_ref[sl].astype(f32)*y).astype(bf)
            gv_ref[sl]=(k_ref[sl].astype(f32)*y).astype(bf)
        return 0
    lax.fori_loop(0,nt,body,0)

V=pl.BlockSpec(memory_space=pltpu.VMEM)
def prep(h,hr,p,g):
    G=h.shape[0]; S=jax.ShapeDtypeStruct
    return pl.pallas_call(prep_kernel,out_shape=(S((G*B,2*LN),bf),S((G*B,2*LN),bf),S((G*B,LN),bf),S((G*B,LN),bf),S((G*B,LN),bf)),
        in_specs=[V]*4,out_specs=(V,)*5,name="prep")(h,hr,p,g)
def mixed(tm,pn,gn,bef,go):
    S=jax.ShapeDtypeStruct
    return pl.pallas_call(mixed_kernel,out_shape=(S(go.shape,bf),S((tm.shape[0]//B,LN),f32)),in_specs=[V]*5,out_specs=(V,)*2,name="mixed")(tm,pn,gn,bef,go)
def back(tb,gn,aft,k,v):
    S=jax.ShapeDtypeStruct
    return pl.pallas_call(back_kernel,out_shape=(S(k.shape,bf),S(k.shape,bf)),in_specs=[V]*5,out_specs=(V,)*2,name="back")(tb,gn,aft,k,v)


def reduce_filter(partial, size):
    index = lax.axis_index("ctx")
    step = 1
    pieces = partial.reshape((size, partial.shape[0] // size) + partial.shape[1:])
    while step < size:
        pairs = [(i, i ^ step) for i in range(size)]
        split = pieces.reshape((pieces.shape[0] // 2, 2) + pieces.shape[1:])
        bit = (index // step) % 2
        keep = lax.dynamic_index_in_dim(split, bit, 1, keepdims=False)
        send = lax.dynamic_index_in_dim(split, 1 - bit, 1, keepdims=False)
        pieces = keep + lax.ppermute(send, "ctx", pairs)
        step *= 2
    return pieces[0]


def shards(query_rows, key_rows, value_rows, grad_out, conv_filter):
    size = lax.axis_size("ctx")
    product = (key_rows.astype(f32) * value_rows.astype(f32)).astype(bf)
    gated = (grad_out.astype(f32) * query_rows.astype(f32)).astype(bf)
    before = lax.ppermute(product, "ctx", [(i, i + 1) for i in range(size - 1)])
    after = lax.ppermute(gated, "ctx", [(i + 1, i) for i in range(size - 1)])
    taps = conv_filter.astype(f32)
    tm, tb, pn, gn, gr = prep(taps, taps[:, ::-1], product, gated)
    grad_query, partial = mixed(tm, pn, gr, before, grad_out)
    own = reduce_filter(partial, size)
    grad_key, grad_value = back(tb, gn, after, key_rows, value_rows)
    scale = 1.0 / math.sqrt(query_rows.shape[0] * size * GSIZE)
    return grad_query, grad_key, grad_value, own[:, ::-1] * scale


def solution(mesh):
    rows = P(("grp", "ctx"), None)
    return jax.shard_map(
        shards,
        mesh=mesh,
        in_specs=(rows, rows, rows, rows, P()),
        out_specs=(rows, rows, rows, rows),
        check_vma=False,
    )
```

time: 200 us -> 90.9 us (0.45)
  the two profiles are of different devices: /device:TPU:15 before, /device:TPU:0 now
where the time goes in v1:
time: 90.9 us; the launch traced here: 90.6 us
  Pallas kernels  52.1 us (57%)
  waiting for transfers between devices  14.2 us (16%)
  starting transfers between devices  13.8 us (15%)
  other arithmetic  6.1 us (7%)
  local copies, waits for them, and re-layouts  3.69 us (4%)
    pallas_call x1, Pallas kernels, mixed(): pl.pallas_call(mixed_kernel, out_shape=(S(go.shape, bf), S((tm.shape[0] /...  22.5 us
    pallas_call x1, Pallas kernels, back(): pl.pallas_call(back_kernel, out_shape=(S(k.shape, bf), S(k.shape, bf)), i...  17.7 us
    ppermute x4, waiting for transfers between devices, reduce_filter(): pieces = keep + lax.ppermute(send, 'ctx', pairs)  14.2 us
    pallas_call x1, Pallas kernels, prep(): pl.pallas_call(prep_kernel, out_shape=(S((G * B, 2 * LN), bf), S((G * B,...  11.9 us
    ppermute x4, starting transfers between devices, reduce_filter(): pieces = keep + lax.ppermute(send, 'ctx', pairs)  10.1 us
    convert_element_type x1, other arithmetic, shards(): gated = (grad_out.astype(f32) * query_rows.astype(f32)).astype(bf)  3.96 us
    ppermute x1, starting transfers between devices, shards(): before = lax.ppermute(product, 'ctx', [(i, i + 1) for i in range(size - 1)])  2.45 us
    unnamed x10, local copies, waits for them, and re-layouts  1.95 us
  transfers between devices with their start and end apart: 6, of which 2 were waited for; matrix products, arithmetic and copies ran while one was open for 3% of the time, Pallas kernels for 33%

profile of v1, /device:TPU:0, one launch (start us, length us, event | category | flops | bytes accessed | tf_op | source)
XLA Modules:
  0.0 90.6 jit_solution(11092884609708776796)
XLA Ops:
  0.6 0.0 copy-start.4
  0.6 4.0 %multiply_convert_fusion = (bf16[128,4096]{1,0:T(8,128)(2,1)}, bf16[128,4096]{1,0:T(8,128)(2,1)S(1)}) fusion(bf16[128,4096]{1,0:T(8,128)(2,1)} %param.5, bf16[128,4096]{1,0:T(8,128)(2,1)} %go_ref.1, bf16[128,4096]{1,0:T(8,128)(2,1)} %v_ref.1, bf16[128,4096]{1,0:T(8,128)(2,1)} %k_ref.1), kind=kLoop, calls=%fused_computation | loop fusion | flops 4194304 | bytes 6291456 | tf_op jit(solution)/shard_map/convert_element_type | solution.py:147
  4.6 0.0 copy-start.1
  4.6 2.5 %collective-permute-start = (bf16[128,4096]{1,0:T(8,128)(2,1)S(1)}, bf16[128,4096]{1,0:T(8,128)(2,1)S(1)}, u32[]{:S(2)}, u32[]{:S(2)}) collective-permute-start(bf16[128,4096]{1,0:T(8,128)(2,1)S(1)} %get-tuple-element.23.p_ref), channel_id=1, source_target_pairs={{0,1},{1,2},{2,3},{3,4},{4,5},{5,6},{6,7},{7,8},{8,9},{9,10},{10,1... | collective-permute-start | bytes 3145736 | tf_op jit(solution)/shard_map/ppermute | solution.py:148
  7.1 0.0 copy-done.4
  7.1 0.7 convert_element_type.21.h_ref
  7.7 0.8 rev.6.hr_ref
  8.5 0.0 copy-done.1
  8.5 11.9 %prep.1 = (bf16[4096,256]{1,0:T(8,128)(2,1)}, bf16[4096,256]{1,0:T(8,128)(2,1)}, bf16[4096,128]{1,0:T(8,128)(2,1)}, bf16[4096,128]{1,0:T(8,128)(2,1)}, bf16[4096,128]{1,0:T(8,128)(2,1)}) custom-call(f32[256,128]{1,0:T(8,128)} %convert_element_type.21.h_ref, f32[256,128]{1,0:T(8,128)} %rev.6.hr_ref, bf16[128,4096]{1,0:T(8,128)(2,1)} %copy-done.1, ...), custom_call_target="tpu_custom_call" | custom-call | tf_op jit(solution)/shard_map/prep/pallas_call | solution.py:119
  20.5 0.0 collective-permute-done.bef_ref
  20.5 0.0 copy-start.3
  20.5 1.0 %copy-done.3 = bf16[128,4096]{1,0:T(8,128)(2,1)} copy-done((bf16[128,4096]{1,0:T(8,128)(2,1)}, bf16[128,4096]{1,0:T(8,128)(2,1)S(1)}, u32[]{:S(2)}) %copy-start.3) | copy-done | bytes 1048600
  21.5 0.0 copy-start
  21.5 22.5 %mixed.1 = (bf16[128,4096]{1,0:T(8,128)(2,1)}, f32[256,128]{1,0:T(8,128)}) custom-call(bf16[4096,256]{1,0:T(8,128)(2,1)} %get-tuple-element.13.tm_ref, bf16[4096,128]{1,0:T(8,128)(2,1)} %get-tuple-element.14.pn_ref, bf16[4096,128]{1,0:T(8,128)(2,1)} %get-tuple-element.15.gr_ref, bf16[128,4096]{1,0:T(8,128)(2,1)} %copy-done.3, bf16[128,4096]{1,0:T(8,128)(2,1)} %go_ref.1), custom_call_target="tpu_custom_call" | custom-call | tf_op jit(solution)/shard_map/mixed/pallas_call | solution.py:123
  44.0 0.8 dynamic-slice_bitcast_fusion
  44.8 2.5 %collective-permute-start.2 = (f32[8,16,128]{2,1,0:T(8,128)S(1)}, f32[8,16,128]{2,1,0:T(8,128)S(1)}, u32[]{:S(2)}, u32[]{:S(2)}) collective-permute-start(f32[8,16,128]{2,1,0:T(8,128)S(1)} %dynamic-slice_bitcast_fusion), channel_id=1, source_target_pairs={{0,1},{1,0},{2,3},{3,2},{4,5},{5,4},{6,7},{7,6},{8,9},{9,8},{10,11... | collective-permute-start | bytes 196616 | tf_op jit(solution)/shard_map/ppermute | solution.py:139
  47.3 0.0 copy-done
  47.3 1.3 %collective-permute-start.1 = (bf16[128,4096]{1,0:T(8,128)(2,1)S(1)}, bf16[128,4096]{1,0:T(8,128)(2,1)S(1)}, u32[]{:S(2)}, u32[]{:S(2)}) collective-permute-start(bf16[128,4096]{1,0:T(8,128)(2,1)S(1)} %copy-done), channel_id=1, source_target_pairs={{1,0},{2,1},{3,2},{4,3},{5,4},{6,5},{7,6},{8,7},{9,8},{10,9},{11,1... | collective-permute-start | bytes 3145736 | tf_op jit(solution)/shard_map/ppermute | solution.py:149
  48.7 0.0 collective-permute-done.2
  48.7 0.9 bitcast_add_fusion
  49.6 2.3 %collective-permute-start.3 = (f32[4,16,128]{2,1,0:T(8,128)S(1)}, f32[4,16,128]{2,1,0:T(8,128)S(1)}, u32[]{:S(2)}, u32[]{:S(2)}) collective-permute-start(f32[4,16,128]{2,1,0:T(8,128)S(1)} %dynamic-slice_bitcast_fusion.1), channel_id=1, source_target_pairs={{0,2},{1,3},{2,0},{3,1},{4,6},{5,7},{6,4},{7,5},{8,10},{9,11},{10,... | collective-permute-start | bytes 98312 | tf_op jit(solution)/shard_map/ppermute | solution.py:139
  51.9 12.5 %collective-permute-done.3 = f32[4,16,128]{2,1,0:T(8,128)S(1)} collective-permute-done((f32[4,16,128]{2,1,0:T(8,128)S(1)}, f32[4,16,128]{2,1,0:T(8,128)S(1)}, u32[]{:S(2)}, u32[]{:S(2)}) %collective-permute-start.3) | collective-permute-done | bytes 32800 | tf_op jit(solution)/shard_map/ppermute | solution.py:139
  64.4 2.2 %collective-permute-start.4 = (f32[2,16,128]{2,1,0:T(8,128)S(1)}, f32[2,16,128]{2,1,0:T(8,128)S(1)}, u32[]{:S(2)}, u32[]{:S(2)}) collective-permute-start(f32[2,16,128]{2,1,0:T(8,128)S(1)} %dynamic-slice_bitcast_fusion.2), channel_id=1, source_target_pairs={{0,4},{1,5},{2,6},{3,7},{4,0},{5,1},{6,2},{7,3},{8,12},{9,13},{10,... | collective-permute-start | bytes 49160 | tf_op jit(solution)/shard_map/ppermute | solution.py:139
  66.6 1.7 %collective-permute-done.4 = f32[2,16,128]{2,1,0:T(8,128)S(1)} collective-permute-done((f32[2,16,128]{2,1,0:T(8,128)S(1)}, f32[2,16,128]{2,1,0:T(8,128)S(1)}, u32[]{:S(2)}, u32[]{:S(2)}) %collective-permute-start.4) | collective-permute-done | bytes 16416 | tf_op jit(solution)/shard_map/ppermute | solution.py:139
  68.3 3.0 %collective-permute-start.5 = (f32[1,16,128]{2,1,0:T(8,128)S(1)}, f32[1,16,128]{2,1,0:T(8,128)S(1)}, u32[]{:S(2)}, u32[]{:S(2)}) collective-permute-start(f32[1,16,128]{2,1,0:T(8,128)S(1)} %constant_dynamic-slice_fusion), channel_id=1, source_target_pairs={{0,8},{1,9},{2,10},{3,11},{4,12},{5,13},{6,14},{7,15},{8,0},{9,1},... | collective-permute-start | bytes 24584 | tf_op jit(solution)/shard_map/ppermute | solution.py:139
  71.3 0.0 collective-permute-done.1.aft_ref
  71.3 0.0 copy-start.2
  71.3 1.0 %copy-done.2 = bf16[128,4096]{1,0:T(8,128)(2,1)} copy-done((bf16[128,4096]{1,0:T(8,128)(2,1)}, bf16[128,4096]{1,0:T(8,128)(2,1)S(1)}, u32[]{:S(2)}) %copy-start.2) | copy-done | bytes 1048600
  72.3 17.7 %back.1 = (bf16[128,4096]{1,0:T(8,128)(2,1)}, bf16[128,4096]{1,0:T(8,128)(2,1)}) custom-call(bf16[4096,256]{1,0:T(8,128)(2,1)} %get-tuple-element.17.tb_ref, bf16[4096,128]{1,0:T(8,128)(2,1)} %get-tuple-element.18.gn_ref, bf16[128,4096]{1,0:T(8,128)(2,1)} %copy-done.2, bf16[128,4096]{1,0:T(8,128)(2,1)} %k_ref.1, bf16[128,4096]{1,0:T(8,128)(2,1)} %v_ref.1), custom_call_target="tpu_custom_call" | custom-call | tf_op jit(solution)/shard_map/back/pallas_call | solution.py:126
  90.0 0.0 collective-permute-done.5
  90.0 0.1 rev.7
  90.0 0.6 broadcast_multiply_fusion
  (6 shorter events, 0.0 us)
Async XLA Ops:
  0.6 6.4 %copy-start.4 = (bf16[256,128]{1,0:T(8,128)(2,1)S(1)}, bf16[256,128]{1,0:T(8,128)(2,1)}, u32[]{:S(2)}) copy-start(bf16[256,128]{1,0:T(8,128)(2,1)} %param.9) | copy-start | bytes 196612
  4.6 3.9 %copy-start.1 = (bf16[128,4096]{1,0:T(8,128)(2,1)}, bf16[128,4096]{1,0:T(8,128)(2,1)S(1)}, u32[]{:S(2)}) copy-start(bf16[128,4096]{1,0:T(8,128)(2,1)S(1)} %get-tuple-element.23.p_ref) | copy-start | bytes 3145732
  4.6 15.9 %collective-permute-start = (bf16[128,4096]{1,0:T(8,128)(2,1)S(1)}, bf16[128,4096]{1,0:T(8,128)(2,1)S(1)}, u32[]{:S(2)}, u32[]{:S(2)}) collective-permute-start(bf16[128,4096]{1,0:T(8,128)(2,1)S(1)} %get-tuple-element.23.p_ref), channel_id=1, source_target_pairs={{0,1},{1,2},{2,3},{3,4},{4,5},{5,6},{6,7},{7,8},{8,9},{9,10},{10,1... | collective-permute-start | bytes 3145736 | tf_op jit(solution)/shard_map/ppermute | solution.py:148
  20.5 1.0 %copy-start.3 = (bf16[128,4096]{1,0:T(8,128)(2,1)}, bf16[128,4096]{1,0:T(8,128)(2,1)S(1)}, u32[]{:S(2)}) copy-start(bf16[128,4096]{1,0:T(8,128)(2,1)S(1)} %collective-permute-done.bef_ref) | copy-start | bytes 3145732
  21.5 25.9 %copy-start = (bf16[128,4096]{1,0:T(8,128)(2,1)S(1)}, bf16[128,4096]{1,0:T(8,128)(2,1)}, u32[]{:S(2)}) copy-start(bf16[128,4096]{1,0:T(8,128)(2,1)} %get-tuple-element.22.g_ref) | copy-start | bytes 3145732
  44.8 3.9 %collective-permute-start.2 = (f32[8,16,128]{2,1,0:T(8,128)S(1)}, f32[8,16,128]{2,1,0:T(8,128)S(1)}, u32[]{:S(2)}, u32[]{:S(2)}) collective-permute-start(f32[8,16,128]{2,1,0:T(8,128)S(1)} %dynamic-slice_bitcast_fusion), channel_id=1, source_target_pairs={{0,1},{1,0},{2,3},{3,2},{4,5},{5,4},{6,7},{7,6},{8,9},{9,8},{10,11... | collective-permute-start | bytes 196616 | tf_op jit(solution)/shard_map/ppermute | solution.py:139
  47.3 24.0 %collective-permute-start.1 = (bf16[128,4096]{1,0:T(8,128)(2,1)S(1)}, bf16[128,4096]{1,0:T(8,128)(2,1)S(1)}, u32[]{:S(2)}, u32[]{:S(2)}) collective-permute-start(bf16[128,4096]{1,0:T(8,128)(2,1)S(1)} %copy-done), channel_id=1, source_target_pairs={{1,0},{2,1},{3,2},{4,3},{5,4},{6,5},{7,6},{8,7},{9,8},{10,9},{11,1... | collective-permute-start | bytes 3145736 | tf_op jit(solution)/shard_map/ppermute | solution.py:149
  49.6 14.8 %collective-permute-start.3 = (f32[4,16,128]{2,1,0:T(8,128)S(1)}, f32[4,16,128]{2,1,0:T(8,128)S(1)}, u32[]{:S(2)}, u32[]{:S(2)}) collective-permute-start(f32[4,16,128]{2,1,0:T(8,128)S(1)} %dynamic-slice_bitcast_fusion.1), channel_id=1, source_target_pairs={{0,2},{1,3},{2,0},{3,1},{4,6},{5,7},{6,4},{7,5},{8,10},{9,11},{10,... | collective-permute-start | bytes 98312 | tf_op jit(solution)/shard_map/ppermute | solution.py:139
  64.4 3.9 %collective-permute-start.4 = (f32[2,16,128]{2,1,0:T(8,128)S(1)}, f32[2,16,128]{2,1,0:T(8,128)S(1)}, u32[]{:S(2)}, u32[]{:S(2)}) collective-permute-start(f32[2,16,128]{2,1,0:T(8,128)S(1)} %dynamic-slice_bitcast_fusion.2), channel_id=1, source_target_pairs={{0,4},{1,5},{2,6},{3,7},{4,0},{5,1},{6,2},{7,3},{8,12},{9,13},{10,... | collective-permute-start | bytes 49160 | tf_op jit(solution)/shard_map/ppermute | solution.py:139
  68.3 21.7 %collective-permute-start.5 = (f32[1,16,128]{2,1,0:T(8,128)S(1)}, f32[1,16,128]{2,1,0:T(8,128)S(1)}, u32[]{:S(2)}, u32[]{:S(2)}) collective-permute-start(f32[1,16,128]{2,1,0:T(8,128)S(1)} %constant_dynamic-slice_fusion), channel_id=1, source_target_pairs={{0,8},{1,9},{2,10},{3,11},{4,12},{5,13},{6,14},{7,15},{8,0},{9,1},... | collective-permute-start | bytes 24584 | tf_op jit(solution)/shard_map/ppermute | solution.py:139
  71.3 1.0 %copy-start.2 = (bf16[128,4096]{1,0:T(8,128)(2,1)}, bf16[128,4096]{1,0:T(8,128)(2,1)S(1)}, u32[]{:S(2)}) copy-start(bf16[128,4096]{1,0:T(8,128)(2,1)S(1)} %collective-permute-done.1.aft_ref) | copy-start | bytes 3145732

commit v2 on v1

v2 whole, which is shorter than its diff:
```python
import math

import jax
import jax.numpy as jnp
from jax import lax
from jax.experimental import pallas as pl
from jax.experimental.pallas import tpu as pltpu
from jax.sharding import PartitionSpec as P

GSIZE = 16
B=32; LN=128; NB=LN//B; LB=LN//NB; SG=LB//GSIZE; H=16
f32=jnp.float32; bf=jnp.bfloat16
def lanes(shape): return lax.broadcasted_iota(jnp.int32, shape, 1)
def subl(shape): return lax.broadcasted_iota(jnp.int32, shape, 0)
def network(vs):
    lane=lanes(vs[0].shape)
    cur=[vs[(-m)%NB] for m in range(NB)]
    bit=1
    while bit<NB:
        mask=(lane & (bit*LB))!=0
        cur=[jnp.where(mask,cur[(m-bit)%NB],cur[m]) for m in range(NB)]
        bit*=2
    return cur
def rot(x,s):
    s%=LN
    return x if s==0 else pltpu.roll(x,s,1)
def to_groups(tile):
    return network([rot(tile[B*a:B*a+B,:],LB*a) for a in range(NB)])
def to_tokens(vs):
    return [rot(e,-LB*a) for a,e in enumerate(network(vs))]
def place(shape,s):
    return (lanes(shape)//LB-s)&(NB-1)
def unfold_back(now,bef,s):
    blk=place(now.shape,s)
    return jnp.concatenate([bef]+[rot(jnp.where(blk<NB-d,now,bef),LB*d) for d in range(NB-1,0,-1)]+[now],0)
def unfold_fwd(now,aft,s):
    blk=place(now.shape,s)
    return jnp.concatenate([now]+[rot(jnp.where(blk>=d,now,aft),-LB*d) for d in range(1,NB)]+[aft],0)
def pick(out,half):
    lane=lanes((B,LN))
    y=out[half*SG*B:half*SG*B+B,half*LN:half*LN+LN]
    for q in range(1,SG):
        y=jnp.where((lane//GSIZE)%SG==q,out[(half*SG+q)*B:(half*SG+q+1)*B,half*LN:half*LN+LN],y)
    return y

def prep_kernel(h_ref,hr_ref,g_ref,tm_ref,tb_ref,gr_ref):
    nt=g_ref.shape[1]//LN
    gt=LN//GSIZE
    lane=lanes((B,LN)); row=subl((B,LN))
    flip=jnp.where(lanes((H,H))+subl((H,H))==H-1,1.,0.).astype(bf)
    lane16=(lanes((H,LN))//GSIZE)%SG
    for j in range(nt):
        gs=to_groups(g_ref[:,j*LN:(j+1)*LN])
        for s in range(NB):
            for half in range(B//H):
                x=jnp.dot(flip,gs[s][half*H:(half+1)*H],preferred_element_type=f32)
                for q in range(SG):
                    r=((j*NB+s)*SG+q)*H
                    gr_ref[r:r+H,half*LN:(half+1)*LN]=jnp.where(lane16==q,x,0.).astype(bf)
        for gi in range(gt):
            g=j*gt+gi
            r0=slice(g*B,(g+1)*B)
            rm=pltpu.roll(jnp.broadcast_to(hr_ref[g:g+1,:],(B,LN)),1,1,stride=1,stride_axis=0)
            tm_ref[r0,0:LN]=jnp.where(lane>row,rm,0.).astype(bf)
            tm_ref[r0,LN:2*LN]=jnp.where(lane<=row,rm,0.).astype(bf)
            rb=pltpu.roll(jnp.broadcast_to(h_ref[g:g+1,:],(B,LN)),0,1,stride=1,stride_axis=0)
            tb_ref[r0,0:LN]=jnp.where(lane>=row,rb,0.).astype(bf)
            tb_ref[r0,LN:2*LN]=jnp.where(lane<row,rb,0.).astype(bf)

def mixed_kernel(tm_ref,p_ref,gr_ref,bef_ref,go_ref,gq_ref,f_ref):
    nt=bef_ref.shape[1]//LN
    gt=LN//GSIZE
    lane=lanes((H,LN)); row=subl((H,LN))
    for j in range(nt):
        co=slice(j*LN,(j+1)*LN)
        now=to_groups(p_ref[:,co]); bef=to_groups(bef_ref[:,co])
        ys=[];fr=[]
        for s in range(0,NB,2):
            us=[unfold_back(now[s+i],bef[s+i],s+i) for i in (0,1)]
            r=(j*gt+s*SG)*B
            y=jnp.dot(tm_ref[r:r+2*SG*B,0:LN+B],jnp.concatenate(us,1),preferred_element_type=f32)
            ys+=[pick(y,0),pick(y,1)]
            for i in (0,1):
                r=(j*gt+(s+i)*SG)*H
                xu=us[i]
                if B==H: rhs=xu
                else: rhs=jnp.concatenate([xu[0:LN+H],xu[H:LN+2*H]],1)
                FF=lax.dot_general(gr_ref[r:r+SG*H,:],rhs,(((1,),(1,)),((),())),preferred_element_type=f32)
                for q in range(SG):
                    F=FF[q*H:(q+1)*H]
                    F2=jnp.concatenate([F[:,LN:LN+H],jnp.zeros((H,LN-H),f32)],1)
                    C=jnp.where(lane+row<=H-1,F2,F[:,:LN])
                    fr.append(jnp.sum(pltpu.roll(C,LN-H,1,stride=1,stride_axis=0),0,keepdims=True))
        f_ref[j*gt:(j+1)*gt,:]=jnp.concatenate(fr,0)
        for a,y in enumerate(to_tokens(ys)):
            gq_ref[B*a:B*a+B,co]=(go_ref[B*a:B*a+B,co].astype(f32)*y).astype(bf)

def back_kernel(tb_ref,g_ref,aft_ref,k_ref,v_ref,gk_ref,gv_ref):
    nt=aft_ref.shape[1]//LN
    gt=LN//GSIZE
    for j in range(nt):
        co=slice(j*LN,(j+1)*LN)
        now=to_groups(g_ref[:,co]); aft=to_groups(aft_ref[:,co])
        ys=[]
        for s in range(0,NB,2):
            xu=jnp.concatenate([unfold_fwd(now[s+i],aft[s+i],s+i) for i in (0,1)],1)
            r=(j*gt+s*SG)*B
            y=jnp.dot(tb_ref[r:r+2*SG*B,0:LN+B],xu,preferred_element_type=f32)
            ys+=[pick(y,0),pick(y,1)]
        for a,y in enumerate(to_tokens(ys)):
            sl=(slice(B*a,B*a+B),co)
            gk_ref[sl]=(v_ref[sl].astype(f32)*y).astype(bf)
            gv_ref[sl]=(k_ref[sl].astype(f32)*y).astype(bf)

STEP=1024
def specs(rows,channels):
    n=channels//STEP
    tok=pl.BlockSpec((rows,STEP),lambda i:(0,i))
    tab=pl.BlockSpec((STEP//GSIZE*B,2*LN),lambda i:(i,0))
    rev=pl.BlockSpec((STEP//GSIZE*H,2*LN),lambda i:(i,0))
    filt=pl.BlockSpec((STEP//GSIZE,LN),lambda i:(i,0))
    return n,tok,tab,filt,rev
def prep(h,hr,g):
    S=jax.ShapeDtypeStruct; G=h.shape[0]
    n,tok,tab,filt,rev=specs(*g.shape)
    t=S((G*B,2*LN),bf)
    return pl.pallas_call(prep_kernel,out_shape=(t,t,S((G*H,2*LN),bf)),grid=(n,),in_specs=[filt,filt,tok],out_specs=(tab,tab,rev),name="prep")(h,hr,g)
def mixed(tm,p,gr,bef,go):
    S=jax.ShapeDtypeStruct
    n,tok,tab,filt,rev=specs(*go.shape)
    return pl.pallas_call(mixed_kernel,out_shape=(S(go.shape,bf),S((tm.shape[0]//B,LN),f32)),grid=(n,),in_specs=[tab,tok,rev,tok,tok],out_specs=(tok,filt),name="mixed")(tm,p,gr,bef,go)
def back(tb,g,aft,k,v):
    S=jax.ShapeDtypeStruct
    n,tok,tab,filt,rev=specs(*k.shape)
    return pl.pallas_call(back_kernel,out_shape=(S(k.shape,bf),S(k.shape,bf)),grid=(n,),in_specs=[tab]+[tok]*4,out_specs=(tok,)*2,name="back")(tb,g,aft,k,v)


def reduce_filter(partial, size):
    index = lax.axis_index("ctx")
    step = 1
    pieces = partial.reshape((size, partial.shape[0] // size) + partial.shape[1:])
    while step < size:
        pairs = [(i, i ^ step) for i in range(size)]
        split = pieces.reshape((pieces.shape[0] // 2, 2) + pieces.shape[1:])
        bit = (index // step) % 2
        keep = lax.dynamic_index_in_dim(split, bit, 1, keepdims=False)
        send = lax.dynamic_index_in_dim(split, 1 - bit, 1, keepdims=False)
        pieces = keep + lax.ppermute(send, "ctx", pairs)
        step *= 2
    return pieces[0]


def shards(query_rows, key_rows, value_rows, grad_out, conv_filter):
    size = lax.axis_size("ctx")
    product = (key_rows.astype(f32) * value_rows.astype(f32)).astype(bf)
    gated = (grad_out.astype(f32) * query_rows.astype(f32)).astype(bf)
    before = lax.ppermute(product, "ctx", [(i, i + 1) for i in range(size - 1)])
    after = lax.ppermute(gated, "ctx", [(i + 1, i) for i in range(size - 1)])
    taps = conv_filter.astype(f32)
    tm, tb, gr = prep(taps, taps[:, ::-1], gated)
    grad_query, partial = mixed(tm, product, gr, before, grad_out)
    own = reduce_filter(partial, size)
    grad_key, grad_value = back(tb, gated, after, key_rows, value_rows)
    scale = 1.0 / math.sqrt(query_rows.shape[0] * size * GSIZE)
    return grad_query, grad_key, grad_value, own[:, ::-1] * scale


def solution(mesh):
    rows = P(("grp", "ctx"), None)
    return jax.shard_map(
        shards,
        mesh=mesh,
        in_specs=(rows, rows, rows, rows, P()),
        out_specs=(rows, rows, rows, rows),
        check_vma=False,
    )
```

time: 90.9 us -> 62.7 us (0.69)
  Pallas kernels: 52.1 us -> 21.2 us
  starting transfers between devices: 13.8 us -> 18.1 us
  local copies, waits for them, and re-layouts: 3.69 us -> 2.74 us
    pallas_call x2, Pallas kernels: 29.6 us -> 13.2 us  [the longest x1 6.72 us: back(): pl.pallas_call(back_kernel, out_shape=(S(k.shape, bf), S(k.shape, bf)), g...]
    pallas_call x1, Pallas kernels: 22.5 us -> 7.92 us  [mixed(): pl.pallas_call(mixed_kernel, out_shape=(S(go.shape, bf), S((tm.shape[0] /...]
    ppermute x4, starting transfers between devices: 10.1 us -> 13.4 us  [reduce_filter(): pieces = keep + lax.ppermute(send, 'ctx', pairs)]
    convert_element_type x1, other arithmetic: 3.96 us -> 1.24 us  [shards(): gated = (grad_out.astype(f32) * query_rows.astype(f32)).astype(bf)]
    convert_element_type x0 -> x1, other arithmetic: none -> 1.94 us  [shards(): product = (key_rows.astype(f32) * value_rows.astype(f32)).astype(bf)]
    ppermute x1, starting transfers between devices: 2.45 us -> 3.41 us  [shards(): before = lax.ppermute(product, 'ctx', [(i, i + 1) for i in range(size - 1)])]
    unnamed x10 -> x12, local copies, waits for them, and re-layouts: 1.95 us -> 1 us
  transfers between devices with their start and end apart: 6 -> 6, of which waited for: 2 -> 2; matrix products, arithmetic and copies ran while one was open for 3% -> 6% of each run, Pallas kernels for 33% -> 21%
where the time goes in v2:
time: 62.7 us; the launch traced here: 62.3 us
  Pallas kernels  21.2 us (34%)
  starting transfers between devices  18.1 us (29%)
  waiting for transfers between devices  14.2 us (23%)
  other arithmetic  5.32 us (8%)
  local copies, waits for them, and re-layouts  2.74 us (4%)
  between operations  0.78 us (1%)
    ppermute x4, waiting for transfers between devices, reduce_filter(): pieces = keep + lax.ppermute(send, 'ctx', pairs)  14.2 us
    ppermute x4, starting transfers between devices, reduce_filter(): pieces = keep + lax.ppermute(send, 'ctx', pairs)  13.4 us
    pallas_call x1, Pallas kernels, mixed(): pl.pallas_call(mixed_kernel, out_shape=(S(go.shape, bf), S((tm.shape[0] /...  7.92 us
    pallas_call x1, Pallas kernels, back(): pl.pallas_call(back_kernel, out_shape=(S(k.shape, bf), S(k.shape, bf)), g...  6.72 us
    pallas_call x1, Pallas kernels, prep(): pl.pallas_call(prep_kernel, out_shape=(t, t, S((G * H, 2 * LN), bf)), gri...  6.53 us
    ppermute x1, starting transfers between devices, shards(): before = lax.ppermute(product, 'ctx', [(i, i + 1) for i in range(size - 1)])  3.41 us
    convert_element_type x1, other arithmetic, shards(): product = (key_rows.astype(f32) * value_rows.astype(f32)).astype(bf)  1.94 us
    ppermute x1, starting transfers between devices, shards(): after = lax.ppermute(gated, 'ctx', [(i + 1, i) for i in range(size - 1)])  1.28 us
  transfers between devices with their start and end apart: 6, of which 2 were waited for; matrix products, arithmetic and copies ran while one was open for 6% of the time, Pallas kernels for 21%

profile of v2, /device:TPU:0, one launch (start us, length us, event | category | flops | bytes accessed | tf_op | source)
XLA Modules:
  0.0 62.3 jit_solution(11753005816807385088)
XLA Ops:
  0.6 0.0 copy-start.5
  0.6 0.0 copy-start.3
  0.7 0.0 copy-start.1
  0.7 1.9 %multiply_convert_fusion.p_ref = bf16[128,4096]{1,0:T(8,128)(2,1)S(1)} fusion(bf16[128,4096]{1,0:T(8,128)(2,1)} %v_ref.1, bf16[128,4096]{1,0:T(8,128)(2,1)} %k_ref.1), kind=kLoop, calls=%fused_computation | loop fusion | flops 2097152 | bytes 3145728 | tf_op jit(solution)/shard_map/convert_element_type | solution.py:155
  2.6 0.0 copy-start.2
  2.6 3.4 %collective-permute-start = (bf16[128,4096]{1,0:T(8,128)(2,1)S(1)}, bf16[128,4096]{1,0:T(8,128)(2,1)}, u32[]{:S(2)}, u32[]{:S(2)}) collective-permute-start(bf16[128,4096]{1,0:T(8,128)(2,1)S(1)} %multiply_convert_fusion.p_ref), channel_id=1, source_target_pairs={{0,1},{1,2},{2,3},{3,4},{4,5},{5,6},{6,7},{7,8},{8,9},{9,10},{10,1... | collective-permute-start | bytes 3145736 | tf_op jit(solution)/shard_map/ppermute | solution.py:157
  6.0 0.0 copy-done.5
  6.0 0.7 %convert_element_type.21.h_ref = f32[256,128]{1,0:T(8,128)} convert(bf16[256,128]{1,0:T(8,128)(2,1)S(1)} %copy-done.5) | non-fusion elementwise | flops 32768 | bytes 196608 | tf_op jit(solution)/shard_map/convert_element_type | solution.py:159
  6.7 0.8 %rev.6.hr_ref = f32[256,128]{1,0:T(8,128)} reverse(bf16[256,128]{1,0:T(8,128)(2,1)S(1)} %copy-done.5), dimensions={1} | reverse | bytes 196608 | tf_op jit(solution)/shard_map/rev | solution.py:160
  7.5 0.0 copy-done.3
  7.5 0.0 copy-done.1
  7.5 1.2 %multiply_convert_fusion.1.g_ref = bf16[128,4096]{1,0:T(8,128)(2,1)} fusion(bf16[128,4096]{1,0:T(8,128)(2,1)S(1)} %copy-done.3, bf16[128,4096]{1,0:T(8,128)(2,1)S(1)} %copy-done.1), kind=kLoop, calls=%fused_computation.1 | loop fusion | flops 2097152 | bytes 3145728 | tf_op jit(solution)/shard_map/convert_element_type | solution.py:156
  8.7 6.5 %prep.1 = (bf16[8192,256]{1,0:T(8,128)(2,1)}, bf16[8192,256]{1,0:T(8,128)(2,1)}, bf16[4096,256]{1,0:T(8,128)(2,1)}) custom-call(f32[256,128]{1,0:T(8,128)} %convert_element_type.21.h_ref, f32[256,128]{1,0:T(8,128)} %rev.6.hr_ref, bf16[128,4096]{1,0:T(8,128)(2,1)} %multiply_convert_fusion.1.g_ref), custom_call_target="tpu_custom_call" | custom-call | tf_op jit(solution)/shard_map/prep/pallas_call | solution.py:127
  15.3 0.0 copy-done.2
  15.3 0.0 collective-permute-done.bef_ref
  15.3 7.9 %mixed.1 = (bf16[128,4096]{1,0:T(8,128)(2,1)}, f32[256,128]{1,0:T(8,128)}) custom-call(bf16[8192,256]{1,0:T(8,128)(2,1)} %get-tuple-element.11.tm_ref, bf16[128,4096]{1,0:T(8,128)(2,1)} %copy-done.2, bf16[4096,256]{1,0:T(8,128)(2,1)} %get-tuple-element.12.gr_ref, bf16[128,4096]{1,0:T(8,128)(2,1)} %collective-permute-done.bef_ref, bf16[128,4096]{1,0:T(8,128)(2,1)} %go_ref.1), custom_call_target="tpu_custom_call" | custom-call | tf_op jit(solution)/shard_map/mixed/pallas_call | solution.py:131
  23.2 0.8 %dynamic-slice_bitcast_fusion = f32[8,16,128]{2,1,0:T(8,128)S(1)} fusion(f32[8,2,16,128]{3,2,1,0:T(8,128)} %bitcast.21, s32[]{:T(128)S(6)} %select_n.60), kind=kLoop, calls=%fused_computation.3 | loop fusion | bytes 131076 | tf_op jit(solution)/shard_map/jit(dynamic_index_in_dim)/squeeze | solution.py:147
  24.1 4.0 %collective-permute-start.2 = (f32[8,16,128]{2,1,0:T(8,128)S(1)}, f32[8,16,128]{2,1,0:T(8,128)S(1)}, u32[]{:S(2)}, u32[]{:S(2)}) collective-permute-start(f32[8,16,128]{2,1,0:T(8,128)S(1)} %dynamic-slice_bitcast_fusion), channel_id=1, source_target_pairs={{0,1},{1,0},{2,3},{3,2},{4,5},{5,4},{6,7},{7,6},{8,9},{9,8},{10,11... | collective-permute-start | bytes 196616 | tf_op jit(solution)/shard_map/ppermute | solution.py:148
  28.1 1.3 %collective-permute-start.1 = (bf16[128,4096]{1,0:T(8,128)(2,1)S(1)}, bf16[128,4096]{1,0:T(8,128)(2,1)S(1)}, u32[]{:S(2)}, u32[]{:S(2)}) collective-permute-start(bf16[128,4096]{1,0:T(8,128)(2,1)S(1)} %copy-done), channel_id=1, source_target_pairs={{1,0},{2,1},{3,2},{4,3},{5,4},{6,5},{7,6},{8,7},{9,8},{10,9},{11,1... | collective-permute-start | bytes 3145736 | tf_op jit(solution)/shard_map/ppermute | solution.py:158
  29.4 0.0 collective-permute-done.2
  29.4 0.9 %bitcast_add_fusion = f32[8,16,128]{2,1,0:T(8,128)S(1)} fusion(f32[8,16,128]{2,1,0:T(8,128)S(1)} %collective-permute-done.2, f32[8,2,16,128]{3,2,1,0:T(8,128)} %bitcast.22, s32[]{:T(128)S(6)} %select_n.59), kind=kLoop, calls=%fused_computation.2 | loop fusion | flops 16384 | bytes 196612 | tf_op jit(solution)/shard_map/add | solution.py:148
  30.3 3.2 %collective-permute-start.3 = (f32[4,16,128]{2,1,0:T(8,128)S(1)}, f32[4,16,128]{2,1,0:T(8,128)S(1)}, u32[]{:S(2)}, u32[]{:S(2)}) collective-permute-start(f32[4,16,128]{2,1,0:T(8,128)S(1)} %dynamic-slice_bitcast_fusion.1), channel_id=1, source_target_pairs={{0,2},{1,3},{2,0},{3,1},{4,6},{5,7},{6,4},{7,5},{8,10},{9,11},{10,... | collective-permute-start | bytes 98312 | tf_op jit(solution)/shard_map/ppermute | solution.py:148
  33.5 12.5 %collective-permute-done.3 = f32[4,16,128]{2,1,0:T(8,128)S(1)} collective-permute-done((f32[4,16,128]{2,1,0:T(8,128)S(1)}, f32[4,16,128]{2,1,0:T(8,128)S(1)}, u32[]{:S(2)}, u32[]{:S(2)}) %collective-permute-start.3) | collective-permute-done | bytes 32800 | tf_op jit(solution)/shard_map/ppermute | solution.py:148
  46.0 3.2 %collective-permute-start.4 = (f32[2,16,128]{2,1,0:T(8,128)S(1)}, f32[2,16,128]{2,1,0:T(8,128)S(1)}, u32[]{:S(2)}, u32[]{:S(2)}) collective-permute-start(f32[2,16,128]{2,1,0:T(8,128)S(1)} %dynamic-slice_bitcast_fusion.2), channel_id=1, source_target_pairs={{0,4},{1,5},{2,6},{3,7},{4,0},{5,1},{6,2},{7,3},{8,12},{9,13},{10,... | collective-permute-start | bytes 49160 | tf_op jit(solution)/shard_map/ppermute | solution.py:148
  49.1 1.7 %collective-permute-done.4 = f32[2,16,128]{2,1,0:T(8,128)S(1)} collective-permute-done((f32[2,16,128]{2,1,0:T(8,128)S(1)}, f32[2,16,128]{2,1,0:T(8,128)S(1)}, u32[]{:S(2)}, u32[]{:S(2)}) %collective-permute-start.4) | collective-permute-done | bytes 16416 | tf_op jit(solution)/shard_map/ppermute | solution.py:148
  50.9 3.0 %collective-permute-start.5 = (f32[1,16,128]{2,1,0:T(8,128)S(1)}, f32[1,16,128]{2,1,0:T(8,128)S(1)}, u32[]{:S(2)}, u32[]{:S(2)}) collective-permute-start(f32[1,16,128]{2,1,0:T(8,128)S(1)} %constant_dynamic-slice_fusion), channel_id=1, source_target_pairs={{0,8},{1,9},{2,10},{3,11},{4,12},{5,13},{6,14},{7,15},{8,0},{9,1},... | collective-permute-start | bytes 24584 | tf_op jit(solution)/shard_map/ppermute | solution.py:148
  53.9 0.0 collective-permute-done.1.aft_ref
  53.9 1.0 %copy-done.4 = bf16[128,4096]{1,0:T(8,128)(2,1)} copy-done((bf16[128,4096]{1,0:T(8,128)(2,1)}, bf16[128,4096]{1,0:T(8,128)(2,1)S(1)}, u32[]{:S(2)}) %copy-start.4) | copy-done | bytes 1048600
  54.9 6.7 %back.1 = (bf16[128,4096]{1,0:T(8,128)(2,1)}, bf16[128,4096]{1,0:T(8,128)(2,1)}) custom-call(bf16[8192,256]{1,0:T(8,128)(2,1)} %get-tuple-element.14.tb_ref, bf16[128,4096]{1,0:T(8,128)(2,1)} %multiply_convert_fusion.1.g_ref, bf16[128,4096]{1,0:T(8,128)(2,1)} %copy-done.4, bf16[128,4096]{1,0:T(8,128)(2,1)} %k_ref.1, bf16[128,4096]{1,0:T(8,128)(2,1)} %v_ref.1), custom_call_target="tpu_custom_call" | custom-call | tf_op jit(solution)/shard_map/back/pallas_call | solution.py:135
  61.6 0.0 collective-permute-done.5
  61.6 0.1 rev.7
  61.7 0.6 broadcast_multiply_fusion
  (9 shorter events, 0.0 us)
Async XLA Ops:
  0.6 5.4 %copy-start.5 = (bf16[256,128]{1,0:T(8,128)(2,1)S(1)}, bf16[256,128]{1,0:T(8,128)(2,1)}, u32[]{:S(2)}) copy-start(bf16[256,128]{1,0:T(8,128)(2,1)} %param.9) | copy-start | bytes 196612
  0.6 6.9 %copy-start.3 = (bf16[128,4096]{1,0:T(8,128)(2,1)S(1)}, bf16[128,4096]{1,0:T(8,128)(2,1)}, u32[]{:S(2)}) copy-start(bf16[128,4096]{1,0:T(8,128)(2,1)} %param.5) | copy-start | bytes 3145732
  0.7 6.8 %copy-start.1 = (bf16[128,4096]{1,0:T(8,128)(2,1)S(1)}, bf16[128,4096]{1,0:T(8,128)(2,1)}, u32[]{:S(2)}) copy-start(bf16[128,4096]{1,0:T(8,128)(2,1)} %go_ref.1) | copy-start | bytes 3145732
  2.6 12.7 %copy-start.2 = (bf16[128,4096]{1,0:T(8,128)(2,1)}, bf16[128,4096]{1,0:T(8,128)(2,1)S(1)}, u32[]{:S(2)}) copy-start(bf16[128,4096]{1,0:T(8,128)(2,1)S(1)} %multiply_convert_fusion.p_ref) | copy-start | bytes 3145732
  2.6 12.7 %collective-permute-start = (bf16[128,4096]{1,0:T(8,128)(2,1)S(1)}, bf16[128,4096]{1,0:T(8,128)(2,1)}, u32[]{:S(2)}, u32[]{:S(2)}) collective-permute-start(bf16[128,4096]{1,0:T(8,128)(2,1)S(1)} %multiply_convert_fusion.p_ref), channel_id=1, source_target_pairs={{0,1},{1,2},{2,3},{3,4},{4,5},{5,6},{6,7},{7,8},{8,9},{9,10},{10,1... | collective-permute-start | bytes 3145736 | tf_op jit(solution)/shard_map/ppermute | solution.py:157
  15.3 12.8 %copy-start = (bf16[128,4096]{1,0:T(8,128)(2,1)S(1)}, bf16[128,4096]{1,0:T(8,128)(2,1)}, u32[]{:S(2)}) copy-start(bf16[128,4096]{1,0:T(8,128)(2,1)} %multiply_convert_fusion.1.g_ref) | copy-start | bytes 3145732
  24.1 5.4 %collective-permute-start.2 = (f32[8,16,128]{2,1,0:T(8,128)S(1)}, f32[8,16,128]{2,1,0:T(8,128)S(1)}, u32[]{:S(2)}, u32[]{:S(2)}) collective-permute-start(f32[8,16,128]{2,1,0:T(8,128)S(1)} %dynamic-slice_bitcast_fusion), channel_id=1, source_target_pairs={{0,1},{1,0},{2,3},{3,2},{4,5},{5,4},{6,7},{7,6},{8,9},{9,8},{10,11... | collective-permute-start | bytes 196616 | tf_op jit(solution)/shard_map/ppermute | solution.py:148
  28.1 25.8 %collective-permute-start.1 = (bf16[128,4096]{1,0:T(8,128)(2,1)S(1)}, bf16[128,4096]{1,0:T(8,128)(2,1)S(1)}, u32[]{:S(2)}, u32[]{:S(2)}) collective-permute-start(bf16[128,4096]{1,0:T(8,128)(2,1)S(1)} %copy-done), channel_id=1, source_target_pairs={{1,0},{2,1},{3,2},{4,3},{5,4},{6,5},{7,6},{8,7},{9,8},{10,9},{11,1... | collective-permute-start | bytes 3145736 | tf_op jit(solution)/shard_map/ppermute | solution.py:158
  30.3 15.6 %collective-permute-start.3 = (f32[4,16,128]{2,1,0:T(8,128)S(1)}, f32[4,16,128]{2,1,0:T(8,128)S(1)}, u32[]{:S(2)}, u32[]{:S(2)}) collective-permute-start(f32[4,16,128]{2,1,0:T(8,128)S(1)} %dynamic-slice_bitcast_fusion.1), channel_id=1, source_target_pairs={{0,2},{1,3},{2,0},{3,1},{4,6},{5,7},{6,4},{7,5},{8,10},{9,11},{10,... | collective-permute-start | bytes 98312 | tf_op jit(solution)/shard_map/ppermute | solution.py:148
  46.0 4.9 %collective-permute-start.4 = (f32[2,16,128]{2,1,0:T(8,128)S(1)}, f32[2,16,128]{2,1,0:T(8,128)S(1)}, u32[]{:S(2)}, u32[]{:S(2)}) collective-permute-start(f32[2,16,128]{2,1,0:T(8,128)S(1)} %dynamic-slice_bitcast_fusion.2), channel_id=1, source_target_pairs={{0,4},{1,5},{2,6},{3,7},{4,0},{5,1},{6,2},{7,3},{8,12},{9,13},{10,... | collective-permute-start | bytes 49160 | tf_op jit(solution)/shard_map/ppermute | solution.py:148
  50.9 10.7 %collective-permute-start.5 = (f32[1,16,128]{2,1,0:T(8,128)S(1)}, f32[1,16,128]{2,1,0:T(8,128)S(1)}, u32[]{:S(2)}, u32[]{:S(2)}) collective-permute-start(f32[1,16,128]{2,1,0:T(8,128)S(1)} %constant_dynamic-slice_fusion), channel_id=1, source_target_pairs={{0,8},{1,9},{2,10},{3,11},{4,12},{5,13},{6,14},{7,15},{8,0},{9,1},... | collective-permute-start | bytes 24584 | tf_op jit(solution)/shard_map/ppermute | solution.py:148
  53.9 1.0 %copy-start.4 = (bf16[128,4096]{1,0:T(8,128)(2,1)}, bf16[128,4096]{1,0:T(8,128)(2,1)S(1)}, u32[]{:S(2)}) copy-start(bf16[128,4096]{1,0:T(8,128)(2,1)S(1)} %collective-permute-done.1.aft_ref) | copy-start | bytes 3145732

commit v3 on v1

v3 whole, which is shorter than its diff:
```python
import math

import jax
import jax.numpy as jnp
from jax import lax
from jax.experimental import pallas as pl
from jax.experimental.pallas import tpu as pltpu
from jax.sharding import PartitionSpec as P

GSIZE = 16
f32 = jnp.float32
bf = jnp.bfloat16
LN = 128
B = 32
NB = LN // B
LB = LN // NB
SG = LB // GSIZE
GT = LN // GSIZE
H = 16
STEP = 1024


def lanes(shape):
    return lax.broadcasted_iota(jnp.int32, shape, 1)


def subl(shape):
    return lax.broadcasted_iota(jnp.int32, shape, 0)


def network(vs):
    lane = lanes(vs[0].shape)
    cur = [vs[(-m) % NB] for m in range(NB)]
    bit = 1
    while bit < NB:
        mask = (lane & (bit * LB)) != 0
        cur = [jnp.where(mask, cur[(m - bit) % NB], cur[m]) for m in range(NB)]
        bit *= 2
    return cur


def rot(x, s):
    s %= LN
    return x if s == 0 else pltpu.roll(x, s, 1)


def to_groups(tile):
    return network([rot(tile[B * a : B * a + B, :], LB * a) for a in range(NB)])


def to_tokens(vs):
    return [rot(e, -LB * a) for a, e in enumerate(network(vs))]


def place(shape, s):
    return (lanes(shape) // LB - s) & (NB - 1)


def unfold_back(now, bef, s):
    blk = place(now.shape, s)
    mid = [rot(jnp.where(blk < NB - d, now, bef), LB * d) for d in range(NB - 1, 0, -1)]
    return jnp.concatenate([bef] + mid + [now], 0)


def unfold_fwd(now, aft, s):
    blk = place(now.shape, s)
    mid = [rot(jnp.where(blk >= d, now, aft), -LB * d) for d in range(1, NB)]
    return jnp.concatenate([now] + mid + [aft], 0)


def pick(out, half):
    lane = lanes((B, LN))
    y = out[half * SG * B : half * SG * B + B, half * LN : half * LN + LN]
    for q in range(1, SG):
        other = out[(half * SG + q) * B : (half * SG + q + 1) * B, half * LN : half * LN + LN]
        y = jnp.where((lane // GSIZE) % SG == q, other, y)
    return y


def column_sums(vs):
    row = subl(vs[0].shape)
    bit = 1
    while len(vs) > 1:
        low = (row & bit) == 0
        vs = [
            jnp.where(low, a, b) + pltpu.roll(jnp.where(low, b, a), 8 - bit, 0)
            for a, b in zip(vs[0::2], vs[1::2])
        ]
        bit *= 2
    return vs[0]


def prep_kernel(h_ref, k_ref, v_ref, p_ref, pn_ref, pr_ref, tm_ref, tb_ref):
    nt = k_ref.shape[1] // LN
    flip = jnp.where(lanes((H, H)) + subl((H, H)) == H - 1, 1.0, 0.0).astype(bf)
    turn = jnp.where(lanes((LN, LN)) + subl((LN, LN)) == LN - 1, 1.0, 0.0).astype(bf)
    h = h_ref[...].astype(f32)
    hr = jnp.dot(h_ref[...], turn, preferred_element_type=f32)
    for j in range(nt):
        co = slice(j * LN, (j + 1) * LN)
        p = (k_ref[:, co].astype(f32) * v_ref[:, co].astype(f32)).astype(bf)
        p_ref[:, co] = p
        ps = to_groups(p)
        for s in range(NB):
            r = (j * NB + s) * B
            pn_ref[r : r + B, :] = ps[s]
            for at in range(0, B, H):
                x = jnp.dot(flip, ps[s][at : at + H], preferred_element_type=f32)
                pr_ref[r + at : r + at + H, :] = x.astype(bf)
        for g in range(j * GT, (j + 1) * GT):
            r0 = slice(g * B, (g + 1) * B)
            rm = jnp.broadcast_to(hr[g : g + 1, :], (B, LN))
            tm_ref[r0, :] = pltpu.roll(rm, 1, 1, stride=1, stride_axis=0).astype(bf)
            rb = jnp.broadcast_to(h[g : g + 1, :], (B, LN))
            tb_ref[r0, :] = pltpu.roll(rb, 0, 1, stride=1, stride_axis=0).astype(bf)


def taps_of(ring, first):
    out = []
    for x in (ring[i : i + B] for i in range(0, ring.shape[0], B)):
        inside = lanes(x.shape) > subl(x.shape) if first else lanes(x.shape) >= subl(x.shape)
        zero = jnp.zeros_like(x)
        out.append(jnp.concatenate([jnp.where(inside, x, zero), jnp.where(inside, zero, x)[:, :B]], 1))
    return jnp.concatenate(out, 0)


def mixed_kernel(t_ref, pn_ref, bef_ref, go_ref, *rest):
    gq_ref = rest[-1]
    nt = bef_ref.shape[1] // LN
    for j in range(nt):
        co = slice(j * LN, (j + 1) * LN)
        bef = to_groups(bef_ref[:, co])
        ys = []
        for s in range(0, NB, 2):
            us = []
            for i in (0, 1):
                r = (j * NB + s + i) * B
                us.append(unfold_back(pn_ref[r : r + B, :], bef[s + i], s + i))
            r = (j * GT + s * SG) * B
            t = taps_of(t_ref[r : r + 2 * SG * B, :], True)
            y = jnp.dot(t, jnp.concatenate(us, 1), preferred_element_type=f32)
            ys += [pick(y, 0), pick(y, 1)]
        for a, y in enumerate(to_tokens(ys)):
            rows = slice(B * a, B * a + B)
            gq_ref[rows, co] = (go_ref[rows, co].astype(f32) * y).astype(bf)


def back_kernel(t_ref, pr_ref, g_ref, aft_ref, k_ref, v_ref, *rest):
    gk_ref, gv_ref, f_ref = rest[-3:]
    nt = aft_ref.shape[1] // LN
    lane, row = lanes((H, LN)), subl((H, LN))
    for j in range(nt):
        co = slice(j * LN, (j + 1) * LN)
        now, aft = to_groups(g_ref[:, co]), to_groups(aft_ref[:, co])
        ys, sums = [], []
        for s in range(0, NB, 2):
            us = [unfold_fwd(now[s + i], aft[s + i], s + i) for i in (0, 1)]
            r = (j * GT + s * SG) * B
            t = taps_of(t_ref[r : r + 2 * SG * B, :], False)
            y = jnp.dot(t, jnp.concatenate(us, 1), preferred_element_type=f32)
            ys += [pick(y, 0), pick(y, 1)]
            for i in (0, 1):
                r = (j * NB + s + i) * B
                rhs = jnp.concatenate([us[i][0 : LN + H], us[i][H : LN + 2 * H]], 1)
                own = jnp.concatenate([pr_ref[r : r + H, :], pr_ref[r + H : r + B, :]], 1)
                part = (lanes(own.shape) // GSIZE) % SG
                lhs = jnp.concatenate([jnp.where(part == q, own, jnp.zeros_like(own)) for q in range(SG)], 0)
                both = lax.dot_general(
                    lhs, rhs, (((1,), (1,)), ((), ())), preferred_element_type=f32
                )
                for q in range(SG):
                    f = both[q * H : (q + 1) * H]
                    edge = jnp.concatenate([f[:, LN : LN + H], jnp.zeros((H, LN - H), f32)], 1)
                    c = jnp.where(lane + row < H - 1, edge, f[:, :LN])
                    c = pltpu.roll(c, LN - H + 1, 1, stride=1, stride_axis=0)
                    sums.append(c[:8] + c[8:])
        f_ref[j * GT : (j + 1) * GT, :] = column_sums(sums)
        for a, y in enumerate(to_tokens(ys)):
            sl = (slice(B * a, B * a + B), co)
            gk_ref[sl] = (v_ref[sl].astype(f32) * y).astype(bf)
            gv_ref[sl] = (k_ref[sl].astype(f32) * y).astype(bf)


def hbm(x):
    return pltpu.with_memory_space_constraint(x, pltpu.HBM)


def tok(start=0):
    return pl.BlockSpec((LN, STEP), lambda i: (0, i + start))


def table(rows, start=0):
    return pl.BlockSpec((STEP // GSIZE * rows, LN), lambda i: (i + start, 0))


def shape(*dims, kind=bf):
    return jax.ShapeDtypeStruct(dims, kind)


def prep(h, k, v):
    groups = h.shape[0]
    t, r = shape(groups * B, LN), shape(groups * H, LN)
    return pl.pallas_call(
        prep_kernel,
        out_shape=(shape(*k.shape), r, r, t, t),
        grid=(k.shape[1] // STEP,),
        in_specs=[table(1), tok(), tok()],
        out_specs=(tok(), table(H), table(H), table(B), table(B)),
        name="prep",
    )(hbm(h), hbm(k), hbm(v))


ANY = pl.BlockSpec(memory_space=pl.ANY)
PARAMS = pltpu.CompilerParams(vmem_limit_bytes=48 << 20)


def mixed(t, pn, bef, go, start, old):
    at = start // STEP
    return pl.pallas_call(
        mixed_kernel,
        out_shape=(shape(*go.shape),),
        grid=(bef.shape[1] // STEP,),
        in_specs=[table(B, at), table(H, at), tok(), tok(at)] + [ANY] * len(old),
        out_specs=(tok(at),),
        input_output_aliases={4 + i: i for i in range(len(old))},
        compiler_params=PARAMS,
        name="mixed",
    )(*(hbm(x) for x in (t, pn)), bef, hbm(go), *old)


def back(t, pr, g, aft, k, v, start, old):
    at = start // STEP
    return pl.pallas_call(
        back_kernel,
        out_shape=(shape(*k.shape), shape(*k.shape), shape(k.shape[1] // GSIZE, LN, kind=f32)),
        grid=(g.shape[1] // STEP,),
        in_specs=[table(B, at), table(H, at), tok(), tok(), tok(at), tok(at)] + [ANY] * len(old),
        out_specs=(tok(at), tok(at), table(1, at)),
        input_output_aliases={6 + i: i for i in range(len(old))},
        compiler_params=PARAMS,
        name="back",
    )(hbm(t), hbm(pr), hbm(g), aft, hbm(k), hbm(v), *old)


def pairs_of(size, step):
    return [(i, i ^ step) for i in range(size)]


def reduce_filter(partial, size):
    index = lax.axis_index("ctx")
    step = 1
    pieces = partial.reshape((size, partial.shape[0] // size) + partial.shape[1:])
    while step < size:
        split = pieces.reshape((pieces.shape[0] // 2, 2) + pieces.shape[1:])
        bit = (index // step) % 2
        keep = lax.dynamic_index_in_dim(split, bit, 1, keepdims=False)
        send = lax.dynamic_index_in_dim(split, 1 - bit, 1, keepdims=False)
        got = lax.ppermute(send, "ctx", pairs_of(size, step))
        pieces = keep + got
        step *= 2
    return pieces[0]


PARTS = 2


def shards(query_rows, key_rows, value_rows, grad_out, conv_filter):
    size = lax.axis_size("ctx")
    channels = key_rows.shape[1]
    width = channels // PARTS
    down = [(i + 1, i) for i in range(size - 1)]
    up = [(i, i + 1) for i in range(size - 1)]
    gated, after = [], []
    for c in range(PARTS):
        cut = slice(c * width, (c + 1) * width)
        gated.append((grad_out[:, cut].astype(f32) * query_rows[:, cut].astype(f32)).astype(bf))
        after.append(lax.ppermute(gated[c], "ctx", down))
    product, pn, pr, tm, tb = prep(conv_filter, key_rows, value_rows)
    before = lax.ppermute(product, "ctx", up)
    old = ()
    for c in range(PARTS):
        old = back(tb, pr, gated[c], after[c], key_rows, value_rows, c * width, old)
    grad_key, grad_value, partial = old
    own = reduce_filter(partial, size)
    (grad_query,) = mixed(tm, pn, before, grad_out, 0, ())
    scale = 1.0 / math.sqrt(query_rows.shape[0] * size * GSIZE)
    return grad_query, grad_key, grad_value, own * scale


def solution(mesh):
    rows = P(("grp", "ctx"), None)

    return jax.shard_map(
        shards,
        mesh=mesh,
        in_specs=(rows, rows, rows, rows, P()),
        out_specs=(rows, rows, rows, rows),
        check_vma=False,
    )
```

time: 90.9 us -> 57.4 us (0.63)
  Pallas kernels: 52.1 us -> 21 us
  starting transfers between devices: 13.8 us -> 27.4 us
  waiting for transfers between devices: 14.2 us -> 5.25 us
  local copies, waits for them, and re-layouts: 3.69 us -> 0.04 us
  other arithmetic: 6.1 us -> 2.53 us
    pallas_call x3 -> x4, Pallas kernels: 52.1 us -> 21 us  [the longest x2 9.45 us: back(): pl.pallas_call(back_kernel, out_shape=(shape(*k.shape), shape(*k.shape),...]
    ppermute x6 -> x7, starting transfers between devices: 13.8 us -> 27.4 us  [the longest x4 22.8 us: reduce_filter(): got = lax.ppermute(send, 'ctx', pairs_of(size, step))]
    ppermute x6 -> x7, waiting for transfers between devices: 14.2 us -> 5.25 us  [the longest x4 5.24 us: reduce_filter(): got = lax.ppermute(send, 'ctx', pairs_of(size, step))]
    convert_element_type x2 -> x1, other arithmetic: 4.63 us -> 1.91 us  [shards(): (grad_out[:, cut].astype(f32) * query_rows[:, cut].astype(f32)).astype(bf)]
    unnamed x10 -> x6, local copies, waits for them, and re-layouts: 1.95 us -> 0.01 us
  transfers between devices with their start and end apart: 6 -> 7, of which waited for: 2 -> 3; matrix products, arithmetic and copies ran while one was open for 3% -> 1% of each run, Pallas kernels for 33% -> 18%
where the time goes in v3:
time: 57.4 us; the launch traced here: 57 us
  starting transfers between devices  27.4 us (48%)
  Pallas kernels  21 us (37%)
  waiting for transfers between devices  5.25 us (9%)
  other arithmetic  2.53 us (4%)
  between operations  0.8 us (1%)
    ppermute x4, starting transfers between devices, reduce_filter(): got = lax.ppermute(send, 'ctx', pairs_of(size, step))  22.8 us
    pallas_call x2, Pallas kernels, back(): pl.pallas_call(back_kernel, out_shape=(shape(*k.shape), shape(*k.shape),...  9.45 us
    pallas_call x1, Pallas kernels, mixed(): pl.pallas_call(mixed_kernel, out_shape=(shape(*go.shape),), grid=(bef.sha...  5.85 us
    pallas_call x1, Pallas kernels, prep(): pl.pallas_call(prep_kernel, out_shape=(shape(*k.shape), r, r, t, t), grid...  5.7 us
    ppermute x4, waiting for transfers between devices, reduce_filter(): got = lax.ppermute(send, 'ctx', pairs_of(size, step))  5.24 us
    ppermute x2, starting transfers between devices, shards(): after.append(lax.ppermute(gated[c], 'ctx', down))  2.58 us
    ppermute x1, starting transfers between devices, shards(): before = lax.ppermute(product, 'ctx', up)  1.99 us
    convert_element_type x1, other arithmetic, shards(): (grad_out[:, cut].astype(f32) * query_rows[:, cut].astype(f32)).astype(bf)  1.91 us
  transfers between devices with their start and end apart: 7, of which 3 were waited for; matrix products, arithmetic and copies ran while one was open for 1% of the time, Pallas kernels for 18%

profile of v3, /device:TPU:0, one launch (start us, length us, event | category | flops | bytes accessed | tf_op | source)
XLA Modules:
  0.0 57.0 jit_solution(8640325757143338107)
XLA Ops:
  0.6 1.9 %multiply_convert_fusion = (bf16[128,2048]{1,0:T(8,128)(2,1)S(1)}, bf16[128,2048]{1,0:T(8,128)(2,1)S(1)}) fusion(bf16[128,4096]{1,0:T(8,128)(2,1)} %param.5, bf16[128,4096]{1,0:T(8,128)(2,1)} %go_ref.1), kind=kLoop, calls=%fused_computation | loop fusion | flops 2097152 | bytes 3145728 | tf_op jit(solution)/shard_map/convert_element_type | solution.py:276
  2.5 0.0 copy-start.1
  2.6 0.0 copy-start
  2.6 1.3 %collective-permute-start.2 = (bf16[128,2048]{1,0:T(8,128)(2,1)S(1)}, bf16[128,2048]{1,0:T(8,128)(2,1)S(1)}, u32[]{:S(2)}, u32[]{:S(2)}) collective-permute-start(bf16[128,2048]{1,0:T(8,128)(2,1)S(1)} %get-tuple-element.26.g_ref), channel_id=1, source_target_pairs={{1,0},{2,1},{3,2},{4,3},{5,4},{6,5},{7,6},{8,7},{9,8},{10,9},{11,1... | collective-permute-start | bytes 1572872 | tf_op jit(solution)/shard_map/ppermute | solution.py:277
  3.9 1.3 %collective-permute-start.1 = (bf16[128,2048]{1,0:T(8,128)(2,1)S(1)}, bf16[128,2048]{1,0:T(8,128)(2,1)S(1)}, u32[]{:S(2)}, u32[]{:S(2)}) collective-permute-start(bf16[128,2048]{1,0:T(8,128)(2,1)S(1)} %get-tuple-element.27.g_ref), channel_id=1, source_target_pairs={{1,0},{2,1},{3,2},{4,3},{5,4},{6,5},{7,6},{8,7},{9,8},{10,9},{11,1... | collective-permute-start | bytes 1572872 | tf_op jit(solution)/shard_map/ppermute | solution.py:277
  5.2 5.7 %prep.1 = (bf16[128,4096]{1,0:T(8,128)(2,1)}, bf16[4096,128]{1,0:T(8,128)(2,1)}, bf16[4096,128]{1,0:T(8,128)(2,1)}, bf16[8192,128]{1,0:T(8,128)(2,1)}, bf16[8192,128]{1,0:T(8,128)(2,1)}) custom-call(bf16[256,128]{1,0:T(8,128)(2,1)} %h_ref.1, bf16[128,4096]{1,0:T(8,128)(2,1)} %k_ref.5, bf16[128,4096]{1,0:T(8,128)(2,1)} %v_ref.5), custom_call_target="tpu_custom_call" | custom-call | tf_op jit(solution)/shard_map/prep/pallas_call | solution.py:203
  10.9 0.0 collective-permute-done.2.aft_ref
  10.9 0.0 copy-done.1
  10.9 4.7 %back.2 = (bf16[128,4096]{1,0:T(8,128)(2,1)}, bf16[128,4096]{1,0:T(8,128)(2,1)}, f32[256,128]{1,0:T(8,128)S(1)}) custom-call(bf16[8192,128]{1,0:T(8,128)(2,1)} %get-tuple-element.18.t_ref, bf16[4096,128]{1,0:T(8,128)(2,1)} %get-tuple-element.19.pr_ref, bf16[128,2048]{1,0:T(8,128)(2,1)} %copy-done.1, bf16[128,2048]{1,0:T(8,128)(2,1)S(1)} %collective-permute-done.2.aft_ref, ...), custom_call_target="tpu_custom_call" | custom-call | tf_op jit(solution)/shard_map/back/pallas_call | solution.py:233
  15.6 0.0 copy-done
  15.6 0.0 collective-permute-done.1.aft_ref
  15.6 0.0 copy-start.2
  15.6 4.8 %back.3 = (bf16[128,4096]{1,0:T(8,128)(2,1)}, bf16[128,4096]{1,0:T(8,128)(2,1)}, f32[256,128]{1,0:T(8,128)S(1)}) custom-call(bf16[8192,128]{1,0:T(8,128)(2,1)} %get-tuple-element.18.t_ref, bf16[4096,128]{1,0:T(8,128)(2,1)} %get-tuple-element.19.pr_ref, bf16[128,2048]{1,0:T(8,128)(2,1)} %copy-done, ...), custom_call_target="tpu_custom_call", output_to_operand_aliasing={{0}: (6, {}), {1}: (7, {}), {2}: (8, {})} | custom-call | tf_op jit(solution)/shard_map/back/pallas_call | solution.py:233
  20.4 4.5 %collective-permute-start.3 = (f32[8,16,128]{2,1,0:T(8,128)S(1)}, f32[8,16,128]{2,1,0:T(8,128)S(1)}, u32[]{:S(2)}, u32[]{:S(2)}) collective-permute-start(f32[8,16,128]{2,1,0:T(8,128)S(1)} %dynamic-slice_bitcast_fusion), channel_id=1, source_target_pairs={{0,1},{1,0},{2,3},{3,2},{4,5},{5,4},{6,7},{7,6},{8,9},{9,8},{10,11... | collective-permute-start | bytes 196616 | tf_op jit(solution)/shard_map/ppermute | solution.py:258
  24.9 0.0 copy-done.2
  24.9 2.0 %collective-permute-start = (bf16[128,4096]{1,0:T(8,128)(2,1)S(1)}, bf16[128,4096]{1,0:T(8,128)(2,1)S(1)}, u32[]{:S(2)}, u32[]{:S(2)}) collective-permute-start(bf16[128,4096]{1,0:T(8,128)(2,1)S(1)} %copy-done.2), channel_id=1, source_target_pairs={{0,1},{1,2},{2,3},{3,4},{4,5},{5,6},{6,7},{7,8},{8,9},{9,10},{10,1... | collective-permute-start | bytes 3145736 | tf_op jit(solution)/shard_map/ppermute | solution.py:279
  26.9 0.0 collective-permute-done.3
  27.0 2.4 %collective-permute-start.4 = (f32[4,16,128]{2,1,0:T(8,128)S(1)}, f32[4,16,128]{2,1,0:T(8,128)S(1)}, u32[]{:S(2)}, u32[]{:S(2)}) collective-permute-start(f32[4,16,128]{2,1,0:T(8,128)S(1)} %dynamic-slice_bitcast_fusion.1), channel_id=1, source_target_pairs={{0,2},{1,3},{2,0},{3,1},{4,6},{5,7},{6,4},{7,5},{8,10},{9,11},{10,... | collective-permute-start | bytes 98312 | tf_op jit(solution)/shard_map/ppermute | solution.py:258
  29.3 1.9 %collective-permute-done.4 = f32[4,16,128]{2,1,0:T(8,128)S(1)} collective-permute-done((f32[4,16,128]{2,1,0:T(8,128)S(1)}, f32[4,16,128]{2,1,0:T(8,128)S(1)}, u32[]{:S(2)}, u32[]{:S(2)}) %collective-permute-start.4) | collective-permute-done | bytes 32800 | tf_op jit(solution)/shard_map/ppermute | solution.py:258
  31.2 12.9 %collective-permute-start.5 = (f32[2,16,128]{2,1,0:T(8,128)S(1)}, f32[2,16,128]{2,1,0:T(8,128)S(1)}, u32[]{:S(2)}, u32[]{:S(2)}) collective-permute-start(f32[2,16,128]{2,1,0:T(8,128)S(1)} %dynamic-slice_bitcast_fusion.2), channel_id=1, source_target_pairs={{0,4},{1,5},{2,6},{3,7},{4,0},{5,1},{6,2},{7,3},{8,12},{9,13},{10,... | collective-permute-start | bytes 49160 | tf_op jit(solution)/shard_map/ppermute | solution.py:258
  44.1 1.7 %collective-permute-done.5 = f32[2,16,128]{2,1,0:T(8,128)S(1)} collective-permute-done((f32[2,16,128]{2,1,0:T(8,128)S(1)}, f32[2,16,128]{2,1,0:T(8,128)S(1)}, u32[]{:S(2)}, u32[]{:S(2)}) %collective-permute-start.5) | collective-permute-done | bytes 16416 | tf_op jit(solution)/shard_map/ppermute | solution.py:258
  45.9 3.0 %collective-permute-start.6 = (f32[1,16,128]{2,1,0:T(8,128)S(1)}, f32[1,16,128]{2,1,0:T(8,128)S(1)}, u32[]{:S(2)}, u32[]{:S(2)}) collective-permute-start(f32[1,16,128]{2,1,0:T(8,128)S(1)} %constant_dynamic-slice_fusion), channel_id=1, source_target_pairs={{0,8},{1,9},{2,10},{3,11},{4,12},{5,13},{6,14},{7,15},{8,0},{9,1},... | collective-permute-start | bytes 24584 | tf_op jit(solution)/shard_map/ppermute | solution.py:258
  48.9 1.6 %collective-permute-done.6 = f32[1,16,128]{2,1,0:T(8,128)S(1)} collective-permute-done((f32[1,16,128]{2,1,0:T(8,128)S(1)}, f32[1,16,128]{2,1,0:T(8,128)S(1)}, u32[]{:S(2)}, u32[]{:S(2)}) %collective-permute-start.6) | collective-permute-done | bytes 8224 | tf_op jit(solution)/shard_map/ppermute | solution.py:258
  50.5 0.6 %multiply_bitcast_fusion = f32[16,128]{1,0:T(8,128)} fusion(f32[1,16,128]{2,1,0:T(8,128)S(1)} %collective-permute-done.6, f32[2,16,128]{2,1,0:T(8,128)S(1)} %bitcast_add_fusion.2, s32[]{:T(128)S(6)} %select_n.71), kind=kLoop, calls=%fused_computation.8 | loop fusion | flops 4096 | bytes 24580 | tf_op jit(solution)/shard_map/mul | solution.py:287
  51.1 0.0 collective-permute-done.bef_ref
  51.1 5.8 %mixed.1 = bf16[128,4096]{1,0:T(8,128)(2,1)} custom-call(bf16[8192,128]{1,0:T(8,128)(2,1)} %get-tuple-element.15.t_ref, bf16[4096,128]{1,0:T(8,128)(2,1)} %get-tuple-element.16.pn_ref, bf16[128,4096]{1,0:T(8,128)(2,1)S(1)} %collective-permute-done.bef_ref, bf16[128,4096]{1,0:T(8,128)(2,1)} %go_ref.1), custom_call_target="tpu_custom_call" | custom-call | tf_op jit(solution)/shard_map/mixed/pallas_call | solution.py:219
  (7 shorter events, 0.1 us)
Async XLA Ops:
  2.5 8.4 %copy-start.1 = (bf16[128,2048]{1,0:T(8,128)(2,1)}, bf16[128,2048]{1,0:T(8,128)(2,1)S(1)}, u32[]{:S(2)}) copy-start(bf16[128,2048]{1,0:T(8,128)(2,1)S(1)} %get-tuple-element.26.g_ref) | copy-start | bytes 1572868
  2.6 13.0 %copy-start = (bf16[128,2048]{1,0:T(8,128)(2,1)}, bf16[128,2048]{1,0:T(8,128)(2,1)S(1)}, u32[]{:S(2)}) copy-start(bf16[128,2048]{1,0:T(8,128)(2,1)S(1)} %get-tuple-element.27.g_ref) | copy-start | bytes 1572868
  2.6 8.3 %collective-permute-start.2 = (bf16[128,2048]{1,0:T(8,128)(2,1)S(1)}, bf16[128,2048]{1,0:T(8,128)(2,1)S(1)}, u32[]{:S(2)}, u32[]{:S(2)}) collective-permute-start(bf16[128,2048]{1,0:T(8,128)(2,1)S(1)} %get-tuple-element.26.g_ref), channel_id=1, source_target_pairs={{1,0},{2,1},{3,2},{4,3},{5,4},{6,5},{7,6},{8,7},{9,8},{10,9},{11,1... | collective-permute-start | bytes 1572872 | tf_op jit(solution)/shard_map/ppermute | solution.py:277
  3.9 11.7 %collective-permute-start.1 = (bf16[128,2048]{1,0:T(8,128)(2,1)S(1)}, bf16[128,2048]{1,0:T(8,128)(2,1)S(1)}, u32[]{:S(2)}, u32[]{:S(2)}) collective-permute-start(bf16[128,2048]{1,0:T(8,128)(2,1)S(1)} %get-tuple-element.27.g_ref), channel_id=1, source_target_pairs={{1,0},{2,1},{3,2},{4,3},{5,4},{6,5},{7,6},{8,7},{9,8},{10,9},{11,1... | collective-permute-start | bytes 1572872 | tf_op jit(solution)/shard_map/ppermute | solution.py:277
  15.6 9.3 %copy-start.2 = (bf16[128,4096]{1,0:T(8,128)(2,1)S(1)}, bf16[128,4096]{1,0:T(8,128)(2,1)}, u32[]{:S(2)}) copy-start(bf16[128,4096]{1,0:T(8,128)(2,1)} %get-tuple-element.17) | copy-start | bytes 3145732
  20.4 6.5 %collective-permute-start.3 = (f32[8,16,128]{2,1,0:T(8,128)S(1)}, f32[8,16,128]{2,1,0:T(8,128)S(1)}, u32[]{:S(2)}, u32[]{:S(2)}) collective-permute-start(f32[8,16,128]{2,1,0:T(8,128)S(1)} %dynamic-slice_bitcast_fusion), channel_id=1, source_target_pairs={{0,1},{1,0},{2,3},{3,2},{4,5},{5,4},{6,7},{7,6},{8,9},{9,8},{10,11... | collective-permute-start | bytes 196616 | tf_op jit(solution)/shard_map/ppermute | solution.py:258
  24.9 26.3 %collective-permute-start = (bf16[128,4096]{1,0:T(8,128)(2,1)S(1)}, bf16[128,4096]{1,0:T(8,128)(2,1)S(1)}, u32[]{:S(2)}, u32[]{:S(2)}) collective-permute-start(bf16[128,4096]{1,0:T(8,128)(2,1)S(1)} %copy-done.2), channel_id=1, source_target_pairs={{0,1},{1,2},{2,3},{3,4},{4,5},{5,6},{6,7},{7,8},{8,9},{9,10},{10,1... | collective-permute-start | bytes 3145736 | tf_op jit(solution)/shard_map/ppermute | solution.py:279
  27.0 4.3 %collective-permute-start.4 = (f32[4,16,128]{2,1,0:T(8,128)S(1)}, f32[4,16,128]{2,1,0:T(8,128)S(1)}, u32[]{:S(2)}, u32[]{:S(2)}) collective-permute-start(f32[4,16,128]{2,1,0:T(8,128)S(1)} %dynamic-slice_bitcast_fusion.1), channel_id=1, source_target_pairs={{0,2},{1,3},{2,0},{3,1},{4,6},{5,7},{6,4},{7,5},{8,10},{9,11},{10,... | collective-permute-start | bytes 98312 | tf_op jit(solution)/shard_map/ppermute | solution.py:258
  31.2 14.6 %collective-permute-start.5 = (f32[2,16,128]{2,1,0:T(8,128)S(1)}, f32[2,16,128]{2,1,0:T(8,128)S(1)}, u32[]{:S(2)}, u32[]{:S(2)}) collective-permute-start(f32[2,16,128]{2,1,0:T(8,128)S(1)} %dynamic-slice_bitcast_fusion.2), channel_id=1, source_target_pairs={{0,4},{1,5},{2,6},{3,7},{4,0},{5,1},{6,2},{7,3},{8,12},{9,13},{10,... | collective-permute-start | bytes 49160 | tf_op jit(solution)/shard_map/ppermute | solution.py:258
  45.9 4.7 %collective-permute-start.6 = (f32[1,16,128]{2,1,0:T(8,128)S(1)}, f32[1,16,128]{2,1,0:T(8,128)S(1)}, u32[]{:S(2)}, u32[]{:S(2)}) collective-permute-start(f32[1,16,128]{2,1,0:T(8,128)S(1)} %constant_dynamic-slice_fusion), channel_id=1, source_target_pairs={{0,8},{1,9},{2,10},{3,11},{4,12},{5,13},{6,14},{7,15},{8,0},{9,1},... | collective-permute-start | bytes 24584 | tf_op jit(solution)/shard_map/ppermute | solution.py:258

commit v4 on v3

--- a/solution.py
+++ b/solution.py
@@ -248,17 +248,19 @@
 
 def reduce_filter(partial, size):
     index = lax.axis_index("ctx")
-    step = 1
-    pieces = partial.reshape((size, partial.shape[0] // size) + partial.shape[1:])
-    while step < size:
-        split = pieces.reshape((pieces.shape[0] // 2, 2) + pieces.shape[1:])
-        bit = (index // step) % 2
-        keep = lax.dynamic_index_in_dim(split, bit, 1, keepdims=False)
-        send = lax.dynamic_index_in_dim(split, 1 - bit, 1, keepdims=False)
-        got = lax.ppermute(send, "ctx", pairs_of(size, step))
+    bits = size.bit_length() - 1
+    order = [b for b in (2, 1) + tuple(range(3, bits)) + (0,) if b < bits]
+    left = list(range(bits - 1, -1, -1))
+    pieces = partial.reshape((2,) * bits + (partial.shape[0] // size, partial.shape[1]))
+    for b in order:
+        axis = left.index(b)
+        bit = (index >> b) & 1
+        keep = lax.dynamic_index_in_dim(pieces, bit, axis, keepdims=False)
+        send = lax.dynamic_index_in_dim(pieces, 1 - bit, axis, keepdims=False)
+        got = lax.ppermute(send, "ctx", pairs_of(size, 1 << b))
         pieces = keep + got
-        step *= 2
-    return pieces[0]
+        left.remove(b)
+    return pieces
 
 
 PARTS = 2

time: 57.4 us -> 56.1 us (0.977)
  starting transfers between devices: 27.4 us -> 25.3 us
  waiting for transfers between devices: 5.25 us -> 6.1 us
    ppermute x4, starting transfers between devices: 22.8 us -> 20.8 us  [reduce_filter(): got = lax.ppermute(send, 'ctx', pairs_of(size, 1 << b))]
    ppermute x4, waiting for transfers between devices: 5.24 us -> 6.1 us  [reduce_filter(): got = lax.ppermute(send, 'ctx', pairs_of(size, 1 << b))]
  transfers between devices with their start and end apart: 7 -> 7, of which waited for: 3 -> 4; matrix products, arithmetic and copies ran while one was open for 1% -> 1% of each run, Pallas kernels for 18% -> 19%
where the time goes in v4:
time: 56.1 us; the launch traced here: 55.8 us
  starting transfers between devices  25.3 us (45%)
  Pallas kernels  21 us (37%)
  waiting for transfers between devices  6.1 us (11%)
  other arithmetic  2.53 us (5%)
  between operations  0.74 us (1%)
    ppermute x4, starting transfers between devices, reduce_filter(): got = lax.ppermute(send, 'ctx', pairs_of(size, 1 << b))  20.8 us
    pallas_call x2, Pallas kernels, back(): pl.pallas_call(back_kernel, out_shape=(shape(*k.shape), shape(*k.shape),...  9.45 us
    ppermute x4, waiting for transfers between devices, reduce_filter(): got = lax.ppermute(send, 'ctx', pairs_of(size, 1 << b))  6.1 us
    pallas_call x1, Pallas kernels, mixed(): pl.pallas_call(mixed_kernel, out_shape=(shape(*go.shape),), grid=(bef.sha...  5.85 us
    pallas_call x1, Pallas kernels, prep(): pl.pallas_call(prep_kernel, out_shape=(shape(*k.shape), r, r, t, t), grid...  5.71 us
    ppermute x2, starting transfers between devices, shards(): after.append(lax.ppermute(gated[c], 'ctx', down))  2.58 us
    ppermute x1, starting transfers between devices, shards(): before = lax.ppermute(product, 'ctx', up)  1.91 us
    convert_element_type x1, other arithmetic, shards(): (grad_out[:, cut].astype(f32) * query_rows[:, cut].astype(f32)).astype(bf)  1.91 us
  transfers between devices with their start and end apart: 7, of which 4 were waited for; matrix products, arithmetic and copies ran while one was open for 1% of the time, Pallas kernels for 19%

profile of v4, /device:TPU:0, one launch (start us, length us, event | category | flops | bytes accessed | tf_op | source)
XLA Modules:
  0.0 55.8 jit_solution(15710048963991672500)
XLA Ops:
  0.6 1.9 %multiply_convert_fusion = (bf16[128,2048]{1,0:T(8,128)(2,1)S(1)}, bf16[128,2048]{1,0:T(8,128)(2,1)S(1)}) fusion(bf16[128,4096]{1,0:T(8,128)(2,1)} %param.5, bf16[128,4096]{1,0:T(8,128)(2,1)} %go_ref.1), kind=kLoop, calls=%fused_computation | loop fusion | flops 2097152 | bytes 3145728 | tf_op jit(solution)/shard_map/convert_element_type | solution.py:278
  2.5 0.0 copy-start.1
  2.6 0.0 copy-start
  2.6 1.3 %collective-permute-start.2 = (bf16[128,2048]{1,0:T(8,128)(2,1)S(1)}, bf16[128,2048]{1,0:T(8,128)(2,1)S(1)}, u32[]{:S(2)}, u32[]{:S(2)}) collective-permute-start(bf16[128,2048]{1,0:T(8,128)(2,1)S(1)} %get-tuple-element.26.g_ref), channel_id=1, source_target_pairs={{1,0},{2,1},{3,2},{4,3},{5,4},{6,5},{7,6},{8,7},{9,8},{10,9},{11,1... | collective-permute-start | bytes 1572872 | tf_op jit(solution)/shard_map/ppermute | solution.py:279
  3.9 1.3 %collective-permute-start.1 = (bf16[128,2048]{1,0:T(8,128)(2,1)S(1)}, bf16[128,2048]{1,0:T(8,128)(2,1)S(1)}, u32[]{:S(2)}, u32[]{:S(2)}) collective-permute-start(bf16[128,2048]{1,0:T(8,128)(2,1)S(1)} %get-tuple-element.27.g_ref), channel_id=1, source_target_pairs={{1,0},{2,1},{3,2},{4,3},{5,4},{6,5},{7,6},{8,7},{9,8},{10,9},{11,1... | collective-permute-start | bytes 1572872 | tf_op jit(solution)/shard_map/ppermute | solution.py:279
  5.2 5.7 %prep.1 = (bf16[128,4096]{1,0:T(8,128)(2,1)}, bf16[4096,128]{1,0:T(8,128)(2,1)}, bf16[4096,128]{1,0:T(8,128)(2,1)}, bf16[8192,128]{1,0:T(8,128)(2,1)}, bf16[8192,128]{1,0:T(8,128)(2,1)}) custom-call(bf16[256,128]{1,0:T(8,128)(2,1)} %h_ref.1, bf16[128,4096]{1,0:T(8,128)(2,1)} %k_ref.5, bf16[128,4096]{1,0:T(8,128)(2,1)} %v_ref.5), custom_call_target="tpu_custom_call" | custom-call | tf_op jit(solution)/shard_map/prep/pallas_call | solution.py:203
  10.9 0.0 collective-permute-done.2.aft_ref
  10.9 0.0 copy-done.1
  10.9 4.7 %back.2 = (bf16[128,4096]{1,0:T(8,128)(2,1)}, bf16[128,4096]{1,0:T(8,128)(2,1)}, f32[256,128]{1,0:T(8,128)S(1)}) custom-call(bf16[8192,128]{1,0:T(8,128)(2,1)} %get-tuple-element.18.t_ref, bf16[4096,128]{1,0:T(8,128)(2,1)} %get-tuple-element.19.pr_ref, bf16[128,2048]{1,0:T(8,128)(2,1)} %copy-done.1, bf16[128,2048]{1,0:T(8,128)(2,1)S(1)} %collective-permute-done.2.aft_ref, ...), custom_call_target="tpu_custom_call" | custom-call | tf_op jit(solution)/shard_map/back/pallas_call | solution.py:233
  15.6 0.0 copy-done
  15.6 0.0 collective-permute-done.1.aft_ref
  15.6 0.0 copy-start.2
  15.6 4.8 %back.3 = (bf16[128,4096]{1,0:T(8,128)(2,1)}, bf16[128,4096]{1,0:T(8,128)(2,1)}, f32[256,128]{1,0:T(8,128)S(1)}) custom-call(bf16[8192,128]{1,0:T(8,128)(2,1)} %get-tuple-element.18.t_ref, bf16[4096,128]{1,0:T(8,128)(2,1)} %get-tuple-element.19.pr_ref, bf16[128,2048]{1,0:T(8,128)(2,1)} %copy-done, ...), custom_call_target="tpu_custom_call", output_to_operand_aliasing={{0}: (6, {}), {1}: (7, {}), {2}: (8, {})} | custom-call | tf_op jit(solution)/shard_map/back/pallas_call | solution.py:233
  20.4 5.8 %collective-permute-start.3 = (f32[2,2,2,16,128]{4,3,2,1,0:T(8,128)S(1)}, f32[2,2,2,16,128]{4,3,2,1,0:T(8,128)S(1)}, u32[]{:S(2)}, u32[]{:S(2)}) collective-permute-start(f32[2,2,2,16,128]{4,3,2,1,0:T(8,128)S(1)} %dynamic-slice_bitcast_fusion), channel_id=1, source_target_pairs={{0,4},{1,5},{2,6},{3,7},{4,0},{5,1},{6,2},{7,3},{8,12},{9,13},{10,... | collective-permute-start | bytes 196616 | tf_op jit(solution)/shard_map/ppermute | solution.py:260
  26.2 0.0 copy-done.2
  26.2 1.9 %collective-permute-start = (bf16[128,4096]{1,0:T(8,128)(2,1)S(1)}, bf16[128,4096]{1,0:T(8,128)(2,1)S(1)}, u32[]{:S(2)}, u32[]{:S(2)}) collective-permute-start(bf16[128,4096]{1,0:T(8,128)(2,1)S(1)} %copy-done.2), channel_id=1, source_target_pairs={{0,1},{1,2},{2,3},{3,4},{4,5},{5,6},{6,7},{7,8},{8,9},{9,10},{10,1... | collective-permute-start | bytes 3145736 | tf_op jit(solution)/shard_map/ppermute | solution.py:281
  28.1 0.7 %collective-permute-done.3 = f32[2,2,2,16,128]{4,3,2,1,0:T(8,128)S(1)} collective-permute-done((f32[2,2,2,16,128]{4,3,2,1,0:T(8,128)S(1)}, f32[2,2,2,16,128]{4,3,2,1,0:T(8,128)S(1)}, u32[]{:S(2)}, u32[]{:S(2)}) %collective-permute-start.3) | collective-permute-done | bytes 65568 | tf_op jit(solution)/shard_map/ppermute | solution.py:260
  28.9 1.6 %collective-permute-start.4 = (f32[2,2,16,128]{3,2,1,0:T(8,128)S(1)}, f32[2,2,16,128]{3,2,1,0:T(8,128)S(1)}, u32[]{:S(2)}, u32[]{:S(2)}) collective-permute-start(f32[2,2,16,128]{3,2,1,0:T(8,128)S(1)} %dynamic-slice_bitcast_fusion.1), channel_id=1, source_target_pairs={{0,2},{1,3},{2,0},{3,1},{4,6},{5,7},{6,4},{7,5},{8,10},{9,11},{10,... | collective-permute-start | bytes 98312 | tf_op jit(solution)/shard_map/ppermute | solution.py:260
  30.6 2.3 %collective-permute-done.4 = f32[2,2,16,128]{3,2,1,0:T(8,128)S(1)} collective-permute-done((f32[2,2,16,128]{3,2,1,0:T(8,128)S(1)}, f32[2,2,16,128]{3,2,1,0:T(8,128)S(1)}, u32[]{:S(2)}, u32[]{:S(2)}) %collective-permute-start.4) | collective-permute-done | bytes 32800 | tf_op jit(solution)/shard_map/ppermute | solution.py:260
  32.9 13.3 %collective-permute-start.5 = (f32[2,16,128]{2,1,0:T(8,128)S(1)}, f32[2,16,128]{2,1,0:T(8,128)S(1)}, u32[]{:S(2)}, u32[]{:S(2)}) collective-permute-start(f32[2,16,128]{2,1,0:T(8,128)S(1)} %dynamic-slice_bitcast_fusion.2), channel_id=1, source_target_pairs={{0,8},{1,9},{2,10},{3,11},{4,12},{5,13},{6,14},{7,15},{8,0},{9,1},... | collective-permute-start | bytes 49160 | tf_op jit(solution)/shard_map/ppermute | solution.py:260
  46.2 1.9 %collective-permute-done.5 = f32[2,16,128]{2,1,0:T(8,128)S(1)} collective-permute-done((f32[2,16,128]{2,1,0:T(8,128)S(1)}, f32[2,16,128]{2,1,0:T(8,128)S(1)}, u32[]{:S(2)}, u32[]{:S(2)}) %collective-permute-start.5) | collective-permute-done | bytes 16416 | tf_op jit(solution)/shard_map/ppermute | solution.py:260
  48.1 0.0 collective-permute-start.6
  48.1 1.2 %collective-permute-done.6 = f32[16,128]{1,0:T(8,128)S(1)} collective-permute-done((f32[16,128]{1,0:T(8,128)S(1)}, f32[16,128]{1,0:T(8,128)S(1)}, u32[]{:S(2)}, u32[]{:S(2)}) %collective-permute-start.6) | collective-permute-done | bytes 8224 | tf_op jit(solution)/shard_map/ppermute | solution.py:260
  49.3 0.6 %fusion = f32[16,128]{1,0:T(8,128)} fusion(f32[16,128]{1,0:T(8,128)S(1)} %collective-permute-done.6, f32[2,16,128]{2,1,0:T(8,128)S(1)} %bitcast_add_fusion.2, s32[]{:T(128)S(6)} %select_n.34), kind=kLoop, calls=%fused_computation.9 | loop fusion | flops 4096 | bytes 24580 | tf_op jit(solution)/shard_map/mul | solution.py:289
  49.9 0.0 collective-permute-done.bef_ref
  49.9 5.8 %mixed.1 = bf16[128,4096]{1,0:T(8,128)(2,1)} custom-call(bf16[8192,128]{1,0:T(8,128)(2,1)} %get-tuple-element.15.t_ref, bf16[4096,128]{1,0:T(8,128)(2,1)} %get-tuple-element.16.pn_ref, bf16[128,4096]{1,0:T(8,128)(2,1)S(1)} %collective-permute-done.bef_ref, bf16[128,4096]{1,0:T(8,128)(2,1)} %go_ref.1), custom_call_target="tpu_custom_call" | custom-call | tf_op jit(solution)/shard_map/mixed/pallas_call | solution.py:219
  (7 shorter events, 0.0 us)
Async XLA Ops:
  2.5 8.3 %copy-start.1 = (bf16[128,2048]{1,0:T(8,128)(2,1)}, bf16[128,2048]{1,0:T(8,128)(2,1)S(1)}, u32[]{:S(2)}) copy-start(bf16[128,2048]{1,0:T(8,128)(2,1)S(1)} %get-tuple-element.26.g_ref) | copy-start | bytes 1572868
  2.6 13.0 %copy-start = (bf16[128,2048]{1,0:T(8,128)(2,1)}, bf16[128,2048]{1,0:T(8,128)(2,1)S(1)}, u32[]{:S(2)}) copy-start(bf16[128,2048]{1,0:T(8,128)(2,1)S(1)} %get-tuple-element.27.g_ref) | copy-start | bytes 1572868
  2.6 8.3 %collective-permute-start.2 = (bf16[128,2048]{1,0:T(8,128)(2,1)S(1)}, bf16[128,2048]{1,0:T(8,128)(2,1)S(1)}, u32[]{:S(2)}, u32[]{:S(2)}) collective-permute-start(bf16[128,2048]{1,0:T(8,128)(2,1)S(1)} %get-tuple-element.26.g_ref), channel_id=1, source_target_pairs={{1,0},{2,1},{3,2},{4,3},{5,4},{6,5},{7,6},{8,7},{9,8},{10,9},{11,1... | collective-permute-start | bytes 1572872 | tf_op jit(solution)/shard_map/ppermute | solution.py:279
  3.9 11.7 %collective-permute-start.1 = (bf16[128,2048]{1,0:T(8,128)(2,1)S(1)}, bf16[128,2048]{1,0:T(8,128)(2,1)S(1)}, u32[]{:S(2)}, u32[]{:S(2)}) collective-permute-start(bf16[128,2048]{1,0:T(8,128)(2,1)S(1)} %get-tuple-element.27.g_ref), channel_id=1, source_target_pairs={{1,0},{2,1},{3,2},{4,3},{5,4},{6,5},{7,6},{8,7},{9,8},{10,9},{11,1... | collective-permute-start | bytes 1572872 | tf_op jit(solution)/shard_map/ppermute | solution.py:279
  15.6 10.6 %copy-start.2 = (bf16[128,4096]{1,0:T(8,128)(2,1)S(1)}, bf16[128,4096]{1,0:T(8,128)(2,1)}, u32[]{:S(2)}) copy-start(bf16[128,4096]{1,0:T(8,128)(2,1)} %get-tuple-element.17) | copy-start | bytes 3145732
  20.4 8.5 %collective-permute-start.3 = (f32[2,2,2,16,128]{4,3,2,1,0:T(8,128)S(1)}, f32[2,2,2,16,128]{4,3,2,1,0:T(8,128)S(1)}, u32[]{:S(2)}, u32[]{:S(2)}) collective-permute-start(f32[2,2,2,16,128]{4,3,2,1,0:T(8,128)S(1)} %dynamic-slice_bitcast_fusion), channel_id=1, source_target_pairs={{0,4},{1,5},{2,6},{3,7},{4,0},{5,1},{6,2},{7,3},{8,12},{9,13},{10,... | collective-permute-start | bytes 196616 | tf_op jit(solution)/shard_map/ppermute | solution.py:260
  26.2 23.7 %collective-permute-start = (bf16[128,4096]{1,0:T(8,128)(2,1)S(1)}, bf16[128,4096]{1,0:T(8,128)(2,1)S(1)}, u32[]{:S(2)}, u32[]{:S(2)}) collective-permute-start(bf16[128,4096]{1,0:T(8,128)(2,1)S(1)} %copy-done.2), channel_id=1, source_target_pairs={{0,1},{1,2},{2,3},{3,4},{4,5},{5,6},{6,7},{7,8},{8,9},{9,10},{10,1... | collective-permute-start | bytes 3145736 | tf_op jit(solution)/shard_map/ppermute | solution.py:281
  28.9 4.0 %collective-permute-start.4 = (f32[2,2,16,128]{3,2,1,0:T(8,128)S(1)}, f32[2,2,16,128]{3,2,1,0:T(8,128)S(1)}, u32[]{:S(2)}, u32[]{:S(2)}) collective-permute-start(f32[2,2,16,128]{3,2,1,0:T(8,128)S(1)} %dynamic-slice_bitcast_fusion.1), channel_id=1, source_target_pairs={{0,2},{1,3},{2,0},{3,1},{4,6},{5,7},{6,4},{7,5},{8,10},{9,11},{10,... | collective-permute-start | bytes 98312 | tf_op jit(solution)/shard_map/ppermute | solution.py:260
  32.9 15.2 %collective-permute-start.5 = (f32[2,16,128]{2,1,0:T(8,128)S(1)}, f32[2,16,128]{2,1,0:T(8,128)S(1)}, u32[]{:S(2)}, u32[]{:S(2)}) collective-permute-start(f32[2,16,128]{2,1,0:T(8,128)S(1)} %dynamic-slice_bitcast_fusion.2), channel_id=1, source_target_pairs={{0,8},{1,9},{2,10},{3,11},{4,12},{5,13},{6,14},{7,15},{8,0},{9,1},... | collective-permute-start | bytes 49160 | tf_op jit(solution)/shard_map/ppermute | solution.py:260
  48.1 1.2 %collective-permute-start.6 = (f32[16,128]{1,0:T(8,128)S(1)}, f32[16,128]{1,0:T(8,128)S(1)}, u32[]{:S(2)}, u32[]{:S(2)}) collective-permute-start(f32[16,128]{1,0:T(8,128)S(1)} %dynamic-slice_bitcast_fusion.3), channel_id=1, source_target_pairs={{0,1},{1,0},{2,3},{3,2},{4,5},{5,4},{6,7},{7,6},{8,9},{9,8},{10,11... | collective-permute-start | bytes 24584 | tf_op jit(solution)/shard_map/ppermute | solution.py:260

commit v5 on v4

--- a/solution.py
+++ b/solution.py
@@ -18,6 +18,7 @@
 GT = LN // GSIZE
 H = 16
 STEP = 1024
+WIDE = 2048
 
 
 def lanes(shape):
@@ -214,18 +215,76 @@
 PARAMS = pltpu.CompilerParams(vmem_limit_bytes=48 << 20)
 
 
-def mixed(t, pn, bef, go, start, old):
-    at = start // STEP
+def block(ref, rows, step):
+    if rows == 0:
+        return ref.at[:, pl.ds(step * WIDE, WIDE)]
+    height = WIDE // GSIZE * rows
+    return ref.at[pl.ds(step * height, height), :]
+
+
+def buffer(steps, rows, kind):
+    dims = (LN, WIDE) if rows == 0 else (WIDE // GSIZE * rows, LN)
+    return pltpu.VMEM((steps,) + dims, kind)
+
+
+def streamed(compute, steps, ins, outs, old=(), limit=None):
+    n_in, n_old, n_out = len(ins), len(old), len(outs)
+
+    def kernel(*refs):
+        sources, refs = refs[:n_in], refs[n_in + n_old :]
+        targets, refs = refs[:n_out], refs[n_out:]
+        held, refs = refs[:n_in], refs[n_in:]
+        made, (in_sem, out_sem) = refs[:n_out], refs[n_out:]
+
+        def load(i, c):
+            source = block(sources[i], ins[i][1], ins[i][2] + c)
+            return pltpu.make_async_copy(source, held[i].at[c], in_sem.at[i, c])
+
+        def save(i, c):
+            target = block(targets[i], outs[i][1], outs[i][2] + c)
+            return pltpu.make_async_copy(made[i].at[c], target, out_sem.at[i, c])
+
+        for c in range(steps):
+            for i in range(n_in):
+                load(i, c).start()
+
+        def one(c, carry):
+            for i in range(n_in):
+                load(i, c).wait()
+            compute(*(x.at[c] for x in held), *(x.at[c] for x in made))
+            for i in range(n_out):
+                save(i, c).start()
+            return carry
+
+        for c in range(steps):
+            one(c, 0)
+        for c in range(steps):
+            for i in range(n_out):
+                save(i, c).wait()
+
+    anywhere = pl.BlockSpec(memory_space=pl.ANY)
     return pl.pallas_call(
+        kernel,
+        out_shape=tuple(x[0] for x in outs),
+        in_specs=[anywhere] * (n_in + n_old),
+        out_specs=(anywhere,) * n_out,
+        scratch_shapes=[buffer(steps, x[1], x[0].dtype) for x in ins]
+        + [buffer(steps, x[1], x[0].dtype) for x in outs]
+        + [pltpu.SemaphoreType.DMA((n_in, steps)), pltpu.SemaphoreType.DMA((n_out, steps))],
+        input_output_aliases={n_in + i: i for i in range(n_old)},
+        compiler_params=pltpu.CompilerParams(vmem_limit_bytes=limit),
+    )(*(x[0] if x[3] else hbm(x[0]) for x in ins), *old)
+
+
+def mixed(t, pn, bef, go):
+    return streamed(
         mixed_kernel,
-        out_shape=(shape(*go.shape),),
-        grid=(bef.shape[1] // STEP,),
-        in_specs=[table(B, at), table(H, at), tok(), tok(at)] + [ANY] * len(old),
-        out_specs=(tok(at),),
-        input_output_aliases={4 + i: i for i in range(len(old))},
-        compiler_params=PARAMS,
-        name="mixed",
-    )(*(hbm(x) for x in (t, pn)), bef, hbm(go), *old)
+        go.shape[1] // WIDE,
+        [(t, B, 0, False), (pn, H, 0, False), (bef, 0, 0, True), (go, 0, 0, False)],
+        [(shape(*go.shape), 0, 0)],
+        (),
+        48 << 20,
+    )
 
 
 def back(t, pr, g, aft, k, v, start, old):
@@ -284,7 +343,7 @@
         old = back(tb, pr, gated[c], after[c], key_rows, value_rows, c * width, old)
     grad_key, grad_value, partial = old
     own = reduce_filter(partial, size)
-    (grad_query,) = mixed(tm, pn, before, grad_out, 0, ())
+    (grad_query,) = mixed(tm, pn, before, grad_out)
     scale = 1.0 / math.sqrt(query_rows.shape[0] * size * GSIZE)
     return grad_query, grad_key, grad_value, own * scale
 

time: 56.1 us -> 55.4 us (0.988)
  Pallas kernels: 21 us -> 20.3 us
    pallas_call x1, Pallas kernels: 5.85 us -> 5.17 us  [streamed(): pl.pallas_call(kernel, out_shape=tuple((x[0] for x in outs)), in_specs=[a...]
where the time goes in v5:
time: 55.4 us; the launch traced here: 55.1 us
  starting transfers between devices  25.3 us (46%)
  Pallas kernels  20.3 us (37%)
  waiting for transfers between devices  6.1 us (11%)
  other arithmetic  2.53 us (5%)
  between operations  0.74 us (1%)
    ppermute x4, starting transfers between devices, reduce_filter(): got = lax.ppermute(send, 'ctx', pairs_of(size, 1 << b))  20.8 us
    pallas_call x2, Pallas kernels, back(): pl.pallas_call(back_kernel, out_shape=(shape(*k.shape), shape(*k.shape),...  9.45 us
    ppermute x4, waiting for transfers between devices, reduce_filter(): got = lax.ppermute(send, 'ctx', pairs_of(size, 1 << b))  6.1 us
    pallas_call x1, Pallas kernels, prep(): pl.pallas_call(prep_kernel, out_shape=(shape(*k.shape), r, r, t, t), grid...  5.71 us
    pallas_call x1, Pallas kernels, streamed(): pl.pallas_call(kernel, out_shape=tuple((x[0] for x in outs)), in_specs=[a...  5.17 us
    ppermute x2, starting transfers between devices, shards(): after.append(lax.ppermute(gated[c], 'ctx', down))  2.58 us
    ppermute x1, starting transfers between devices, shards(): before = lax.ppermute(product, 'ctx', up)  1.91 us
    convert_element_type x1, other arithmetic, shards(): (grad_out[:, cut].astype(f32) * query_rows[:, cut].astype(f32)).astype(bf)  1.91 us
  transfers between devices with their start and end apart: 7, of which 4 were waited for; matrix products, arithmetic and copies ran while one was open for 1% of the time, Pallas kernels for 19%

profile of v5, /device:TPU:0, one launch (start us, length us, event | category | flops | bytes accessed | tf_op | source)
XLA Modules:
  0.0 55.1 jit_solution(5306082370134774080)
XLA Ops:
  0.6 1.9 %multiply_convert_fusion = (bf16[128,2048]{1,0:T(8,128)(2,1)S(1)}, bf16[128,2048]{1,0:T(8,128)(2,1)S(1)}) fusion(bf16[128,4096]{1,0:T(8,128)(2,1)} %param.5, bf16[128,4096]{1,0:T(8,128)(2,1)} %refs_3_.1), kind=kLoop, calls=%fused_computation | loop fusion | flops 2097152 | bytes 3145728 | tf_op jit(solution)/shard_map/convert_element_type | solution.py:337
  2.5 0.0 copy-start.1
  2.6 0.0 copy-start
  2.6 1.3 %collective-permute-start.2 = (bf16[128,2048]{1,0:T(8,128)(2,1)S(1)}, bf16[128,2048]{1,0:T(8,128)(2,1)S(1)}, u32[]{:S(2)}, u32[]{:S(2)}) collective-permute-start(bf16[128,2048]{1,0:T(8,128)(2,1)S(1)} %get-tuple-element.26.g_ref), channel_id=1, source_target_pairs={{1,0},{2,1},{3,2},{4,3},{5,4},{6,5},{7,6},{8,7},{9,8},{10,9},{11,1... | collective-permute-start | bytes 1572872 | tf_op jit(solution)/shard_map/ppermute | solution.py:338
  3.9 1.3 %collective-permute-start.1 = (bf16[128,2048]{1,0:T(8,128)(2,1)S(1)}, bf16[128,2048]{1,0:T(8,128)(2,1)S(1)}, u32[]{:S(2)}, u32[]{:S(2)}) collective-permute-start(bf16[128,2048]{1,0:T(8,128)(2,1)S(1)} %get-tuple-element.27.g_ref), channel_id=1, source_target_pairs={{1,0},{2,1},{3,2},{4,3},{5,4},{6,5},{7,6},{8,7},{9,8},{10,9},{11,1... | collective-permute-start | bytes 1572872 | tf_op jit(solution)/shard_map/ppermute | solution.py:338
  5.2 5.7 %prep.1 = (bf16[128,4096]{1,0:T(8,128)(2,1)}, bf16[4096,128]{1,0:T(8,128)(2,1)}, bf16[4096,128]{1,0:T(8,128)(2,1)}, bf16[8192,128]{1,0:T(8,128)(2,1)}, bf16[8192,128]{1,0:T(8,128)(2,1)}) custom-call(bf16[256,128]{1,0:T(8,128)(2,1)} %h_ref.1, bf16[128,4096]{1,0:T(8,128)(2,1)} %k_ref.5, bf16[128,4096]{1,0:T(8,128)(2,1)} %v_ref.5), custom_call_target="tpu_custom_call" | custom-call | tf_op jit(solution)/shard_map/prep/pallas_call | solution.py:204
  10.9 0.0 collective-permute-done.2.aft_ref
  10.9 0.0 copy-done.1
  10.9 4.7 %back.2 = (bf16[128,4096]{1,0:T(8,128)(2,1)}, bf16[128,4096]{1,0:T(8,128)(2,1)}, f32[256,128]{1,0:T(8,128)S(1)}) custom-call(bf16[8192,128]{1,0:T(8,128)(2,1)} %get-tuple-element.18.t_ref, bf16[4096,128]{1,0:T(8,128)(2,1)} %get-tuple-element.19.pr_ref, bf16[128,2048]{1,0:T(8,128)(2,1)} %copy-done.1, bf16[128,2048]{1,0:T(8,128)(2,1)S(1)} %collective-permute-done.2.aft_ref, ...), custom_call_target="tpu_custom_call" | custom-call | tf_op jit(solution)/shard_map/back/pallas_call | solution.py:292
  15.6 0.0 copy-done
  15.6 0.0 collective-permute-done.1.aft_ref
  15.6 0.0 copy-start.2
  15.6 4.8 %back.3 = (bf16[128,4096]{1,0:T(8,128)(2,1)}, bf16[128,4096]{1,0:T(8,128)(2,1)}, f32[256,128]{1,0:T(8,128)S(1)}) custom-call(bf16[8192,128]{1,0:T(8,128)(2,1)} %get-tuple-element.18.t_ref, bf16[4096,128]{1,0:T(8,128)(2,1)} %get-tuple-element.19.pr_ref, bf16[128,2048]{1,0:T(8,128)(2,1)} %copy-done, ...), custom_call_target="tpu_custom_call", output_to_operand_aliasing={{0}: (6, {}), {1}: (7, {}), {2}: (8, {})} | custom-call | tf_op jit(solution)/shard_map/back/pallas_call | solution.py:292
  20.4 5.8 %collective-permute-start.3 = (f32[2,2,2,16,128]{4,3,2,1,0:T(8,128)S(1)}, f32[2,2,2,16,128]{4,3,2,1,0:T(8,128)S(1)}, u32[]{:S(2)}, u32[]{:S(2)}) collective-permute-start(f32[2,2,2,16,128]{4,3,2,1,0:T(8,128)S(1)} %dynamic-slice_bitcast_fusion), channel_id=1, source_target_pairs={{0,4},{1,5},{2,6},{3,7},{4,0},{5,1},{6,2},{7,3},{8,12},{9,13},{10,... | collective-permute-start | bytes 196616 | tf_op jit(solution)/shard_map/ppermute | solution.py:319
  26.2 0.0 copy-done.2
  26.2 1.9 %collective-permute-start = (bf16[128,4096]{1,0:T(8,128)(2,1)S(1)}, bf16[128,4096]{1,0:T(8,128)(2,1)S(1)}, u32[]{:S(2)}, u32[]{:S(2)}) collective-permute-start(bf16[128,4096]{1,0:T(8,128)(2,1)S(1)} %copy-done.2), channel_id=1, source_target_pairs={{0,1},{1,2},{2,3},{3,4},{4,5},{5,6},{6,7},{7,8},{8,9},{9,10},{10,1... | collective-permute-start | bytes 3145736 | tf_op jit(solution)/shard_map/ppermute | solution.py:340
  28.1 0.7 %collective-permute-done.3 = f32[2,2,2,16,128]{4,3,2,1,0:T(8,128)S(1)} collective-permute-done((f32[2,2,2,16,128]{4,3,2,1,0:T(8,128)S(1)}, f32[2,2,2,16,128]{4,3,2,1,0:T(8,128)S(1)}, u32[]{:S(2)}, u32[]{:S(2)}) %collective-permute-start.3) | collective-permute-done | bytes 65568 | tf_op jit(solution)/shard_map/ppermute | solution.py:319
  28.9 1.6 %collective-permute-start.4 = (f32[2,2,16,128]{3,2,1,0:T(8,128)S(1)}, f32[2,2,16,128]{3,2,1,0:T(8,128)S(1)}, u32[]{:S(2)}, u32[]{:S(2)}) collective-permute-start(f32[2,2,16,128]{3,2,1,0:T(8,128)S(1)} %dynamic-slice_bitcast_fusion.1), channel_id=1, source_target_pairs={{0,2},{1,3},{2,0},{3,1},{4,6},{5,7},{6,4},{7,5},{8,10},{9,11},{10,... | collective-permute-start | bytes 98312 | tf_op jit(solution)/shard_map/ppermute | solution.py:319
  30.6 2.3 %collective-permute-done.4 = f32[2,2,16,128]{3,2,1,0:T(8,128)S(1)} collective-permute-done((f32[2,2,16,128]{3,2,1,0:T(8,128)S(1)}, f32[2,2,16,128]{3,2,1,0:T(8,128)S(1)}, u32[]{:S(2)}, u32[]{:S(2)}) %collective-permute-start.4) | collective-permute-done | bytes 32800 | tf_op jit(solution)/shard_map/ppermute | solution.py:319
  32.9 13.3 %collective-permute-start.5 = (f32[2,16,128]{2,1,0:T(8,128)S(1)}, f32[2,16,128]{2,1,0:T(8,128)S(1)}, u32[]{:S(2)}, u32[]{:S(2)}) collective-permute-start(f32[2,16,128]{2,1,0:T(8,128)S(1)} %dynamic-slice_bitcast_fusion.2), channel_id=1, source_target_pairs={{0,8},{1,9},{2,10},{3,11},{4,12},{5,13},{6,14},{7,15},{8,0},{9,1},... | collective-permute-start | bytes 49160 | tf_op jit(solution)/shard_map/ppermute | solution.py:319
  46.2 1.9 %collective-permute-done.5 = f32[2,16,128]{2,1,0:T(8,128)S(1)} collective-permute-done((f32[2,16,128]{2,1,0:T(8,128)S(1)}, f32[2,16,128]{2,1,0:T(8,128)S(1)}, u32[]{:S(2)}, u32[]{:S(2)}) %collective-permute-start.5) | collective-permute-done | bytes 16416 | tf_op jit(solution)/shard_map/ppermute | solution.py:319
  48.1 0.0 collective-permute-start.6
  48.1 1.2 %collective-permute-done.6 = f32[16,128]{1,0:T(8,128)S(1)} collective-permute-done((f32[16,128]{1,0:T(8,128)S(1)}, f32[16,128]{1,0:T(8,128)S(1)}, u32[]{:S(2)}, u32[]{:S(2)}) %collective-permute-start.6) | collective-permute-done | bytes 8224 | tf_op jit(solution)/shard_map/ppermute | solution.py:319
  49.3 0.6 %fusion = f32[16,128]{1,0:T(8,128)} fusion(f32[16,128]{1,0:T(8,128)S(1)} %collective-permute-done.6, f32[2,16,128]{2,1,0:T(8,128)S(1)} %bitcast_add_fusion.2, s32[]{:T(128)S(6)} %select_n.34), kind=kLoop, calls=%fused_computation.9 | loop fusion | flops 4096 | bytes 24580 | tf_op jit(solution)/shard_map/mul | solution.py:348
  49.9 0.0 collective-permute-done.refs_2_
  49.9 5.2 %shard_map.84 = bf16[128,4096]{1,0:T(8,128)(2,1)} custom-call(bf16[8192,128]{1,0:T(8,128)(2,1)} %get-tuple-element.15.refs_0_, bf16[4096,128]{1,0:T(8,128)(2,1)} %get-tuple-element.16.refs_1_, bf16[128,4096]{1,0:T(8,128)(2,1)S(1)} %collective-permute-done.refs_2_, bf16[128,4096]{1,0:T(8,128)(2,1)} %refs_3_.1), custom_call_target="tpu_custom_call" | custom-call | tf_op jit(solution)/shard_map/pallas_call | solution.py:266
  (7 shorter events, 0.0 us)
Async XLA Ops:
  2.5 8.3 %copy-start.1 = (bf16[128,2048]{1,0:T(8,128)(2,1)}, bf16[128,2048]{1,0:T(8,128)(2,1)S(1)}, u32[]{:S(2)}) copy-start(bf16[128,2048]{1,0:T(8,128)(2,1)S(1)} %get-tuple-element.26.g_ref) | copy-start | bytes 1572868
  2.6 13.0 %copy-start = (bf16[128,2048]{1,0:T(8,128)(2,1)}, bf16[128,2048]{1,0:T(8,128)(2,1)S(1)}, u32[]{:S(2)}) copy-start(bf16[128,2048]{1,0:T(8,128)(2,1)S(1)} %get-tuple-element.27.g_ref) | copy-start | bytes 1572868
  2.6 8.3 %collective-permute-start.2 = (bf16[128,2048]{1,0:T(8,128)(2,1)S(1)}, bf16[128,2048]{1,0:T(8,128)(2,1)S(1)}, u32[]{:S(2)}, u32[]{:S(2)}) collective-permute-start(bf16[128,2048]{1,0:T(8,128)(2,1)S(1)} %get-tuple-element.26.g_ref), channel_id=1, source_target_pairs={{1,0},{2,1},{3,2},{4,3},{5,4},{6,5},{7,6},{8,7},{9,8},{10,9},{11,1... | collective-permute-start | bytes 1572872 | tf_op jit(solution)/shard_map/ppermute | solution.py:338
  3.9 11.7 %collective-permute-start.1 = (bf16[128,2048]{1,0:T(8,128)(2,1)S(1)}, bf16[128,2048]{1,0:T(8,128)(2,1)S(1)}, u32[]{:S(2)}, u32[]{:S(2)}) collective-permute-start(bf16[128,2048]{1,0:T(8,128)(2,1)S(1)} %get-tuple-element.27.g_ref), channel_id=1, source_target_pairs={{1,0},{2,1},{3,2},{4,3},{5,4},{6,5},{7,6},{8,7},{9,8},{10,9},{11,1... | collective-permute-start | bytes 1572872 | tf_op jit(solution)/shard_map/ppermute | solution.py:338
  15.6 10.6 %copy-start.2 = (bf16[128,4096]{1,0:T(8,128)(2,1)S(1)}, bf16[128,4096]{1,0:T(8,128)(2,1)}, u32[]{:S(2)}) copy-start(bf16[128,4096]{1,0:T(8,128)(2,1)} %get-tuple-element.17) | copy-start | bytes 3145732
  20.4 8.5 %collective-permute-start.3 = (f32[2,2,2,16,128]{4,3,2,1,0:T(8,128)S(1)}, f32[2,2,2,16,128]{4,3,2,1,0:T(8,128)S(1)}, u32[]{:S(2)}, u32[]{:S(2)}) collective-permute-start(f32[2,2,2,16,128]{4,3,2,1,0:T(8,128)S(1)} %dynamic-slice_bitcast_fusion), channel_id=1, source_target_pairs={{0,4},{1,5},{2,6},{3,7},{4,0},{5,1},{6,2},{7,3},{8,12},{9,13},{10,... | collective-permute-start | bytes 196616 | tf_op jit(solution)/shard_map/ppermute | solution.py:319
  26.2 23.7 %collective-permute-start = (bf16[128,4096]{1,0:T(8,128)(2,1)S(1)}, bf16[128,4096]{1,0:T(8,128)(2,1)S(1)}, u32[]{:S(2)}, u32[]{:S(2)}) collective-permute-start(bf16[128,4096]{1,0:T(8,128)(2,1)S(1)} %copy-done.2), channel_id=1, source_target_pairs={{0,1},{1,2},{2,3},{3,4},{4,5},{5,6},{6,7},{7,8},{8,9},{9,10},{10,1... | collective-permute-start | bytes 3145736 | tf_op jit(solution)/shard_map/ppermute | solution.py:340
  28.9 4.0 %collective-permute-start.4 = (f32[2,2,16,128]{3,2,1,0:T(8,128)S(1)}, f32[2,2,16,128]{3,2,1,0:T(8,128)S(1)}, u32[]{:S(2)}, u32[]{:S(2)}) collective-permute-start(f32[2,2,16,128]{3,2,1,0:T(8,128)S(1)} %dynamic-slice_bitcast_fusion.1), channel_id=1, source_target_pairs={{0,2},{1,3},{2,0},{3,1},{4,6},{5,7},{6,4},{7,5},{8,10},{9,11},{10,... | collective-permute-start | bytes 98312 | tf_op jit(solution)/shard_map/ppermute | solution.py:319
  32.9 15.2 %collective-permute-start.5 = (f32[2,16,128]{2,1,0:T(8,128)S(1)}, f32[2,16,128]{2,1,0:T(8,128)S(1)}, u32[]{:S(2)}, u32[]{:S(2)}) collective-permute-start(f32[2,16,128]{2,1,0:T(8,128)S(1)} %dynamic-slice_bitcast_fusion.2), channel_id=1, source_target_pairs={{0,8},{1,9},{2,10},{3,11},{4,12},{5,13},{6,14},{7,15},{8,0},{9,1},... | collective-permute-start | bytes 49160 | tf_op jit(solution)/shard_map/ppermute | solution.py:319
  48.1 1.2 %collective-permute-start.6 = (f32[16,128]{1,0:T(8,128)S(1)}, f32[16,128]{1,0:T(8,128)S(1)}, u32[]{:S(2)}, u32[]{:S(2)}) collective-permute-start(f32[16,128]{1,0:T(8,128)S(1)} %dynamic-slice_bitcast_fusion.3), channel_id=1, source_target_pairs={{0,1},{1,0},{2,3},{3,2},{4,5},{5,4},{6,7},{7,6},{8,9},{9,8},{10,11... | collective-permute-start | bytes 24584 | tf_op jit(solution)/shard_map/ppermute | solution.py:319

commit v6 on v5

--- a/solution.py
+++ b/solution.py
@@ -146,8 +146,17 @@
             gq_ref[rows, co] = (go_ref[rows, co].astype(f32) * y).astype(bf)
 
 
-def back_kernel(t_ref, pr_ref, g_ref, aft_ref, k_ref, v_ref, *rest):
-    gk_ref, gv_ref, f_ref = rest[-3:]
+def back_kernel(refs, sums_too, rows_too):
+    if rows_too:
+        t_ref, refs = refs[0], refs[1:]
+    if sums_too:
+        pr_ref, refs = refs[0], refs[1:]
+    g_ref, aft_ref = refs[:2]
+    if rows_too:
+        k_ref, v_ref = refs[2:4]
+        gk_ref, gv_ref = refs[-3:-1] if sums_too else refs[-2:]
+    if sums_too:
+        f_ref = refs[-1]
     nt = aft_ref.shape[1] // LN
     lane, row = lanes((H, LN)), subl((H, LN))
     for j in range(nt):
@@ -156,11 +165,12 @@
         ys, sums = [], []
         for s in range(0, NB, 2):
             us = [unfold_fwd(now[s + i], aft[s + i], s + i) for i in (0, 1)]
-            r = (j * GT + s * SG) * B
-            t = taps_of(t_ref[r : r + 2 * SG * B, :], False)
-            y = jnp.dot(t, jnp.concatenate(us, 1), preferred_element_type=f32)
-            ys += [pick(y, 0), pick(y, 1)]
-            for i in (0, 1):
+            if rows_too:
+                r = (j * GT + s * SG) * B
+                t = taps_of(t_ref[r : r + 2 * SG * B, :], False)
+                y = jnp.dot(t, jnp.concatenate(us, 1), preferred_element_type=f32)
+                ys += [pick(y, 0), pick(y, 1)]
+            for i in (0, 1) if sums_too else ():
                 r = (j * NB + s + i) * B
                 rhs = jnp.concatenate([us[i][0 : LN + H], us[i][H : LN + 2 * H]], 1)
                 own = jnp.concatenate([pr_ref[r : r + H, :], pr_ref[r + H : r + B, :]], 1)
@@ -175,8 +185,9 @@
                     c = jnp.where(lane + row < H - 1, edge, f[:, :LN])
                     c = pltpu.roll(c, LN - H + 1, 1, stride=1, stride_axis=0)
                     sums.append(c[:8] + c[8:])
-        f_ref[j * GT : (j + 1) * GT, :] = column_sums(sums)
-        for a, y in enumerate(to_tokens(ys)):
+        if sums_too:
+            f_ref[j * GT : (j + 1) * GT, :] = column_sums(sums)
+        for a, y in enumerate(to_tokens(ys)) if rows_too else ():
             sl = (slice(B * a, B * a + B), co)
             gk_ref[sl] = (v_ref[sl].astype(f32) * y).astype(bf)
             gv_ref[sl] = (k_ref[sl].astype(f32) * y).astype(bf)
@@ -287,18 +298,27 @@
     )
 
 
-def back(t, pr, g, aft, k, v, start, old):
+def back(t, pr, g, aft, k, v, start, old, sums_too=True, rows_too=True):
     at = start // STEP
+    ins = [(hbm(t), table(B, at))] if rows_too else []
+    ins += [(hbm(pr), table(H, at))] if sums_too else []
+    ins += [(hbm(g), tok()), (aft, tok())]
+    ins += [(hbm(k), tok(at)), (hbm(v), tok(at))] if rows_too else []
+    outs = [(shape(*k.shape), tok(at))] * 2 if rows_too else []
+    if sums_too:
+        outs += [(shape(k.shape[1] // GSIZE, LN, kind=f32), table(1, at))]
+    count = len(ins)
+    ins += [(x, ANY) for x in old]
     return pl.pallas_call(
-        back_kernel,
-        out_shape=(shape(*k.shape), shape(*k.shape), shape(k.shape[1] // GSIZE, LN, kind=f32)),
+        lambda *refs: back_kernel(refs, sums_too, rows_too),
+        out_shape=tuple(x[0] for x in outs),
         grid=(g.shape[1] // STEP,),
-        in_specs=[table(B, at), table(H, at), tok(), tok(), tok(at), tok(at)] + [ANY] * len(old),
-        out_specs=(tok(at), tok(at), table(1, at)),
-        input_output_aliases={6 + i: i for i in range(len(old))},
+        in_specs=[x[1] for x in ins],
+        out_specs=tuple(x[1] for x in outs),
+        input_output_aliases={count + i: i for i in range(len(old))},
         compiler_params=PARAMS,
         name="back",
-    )(hbm(t), hbm(pr), hbm(g), aft, hbm(k), hbm(v), *old)
+    )(*(x[0] for x in ins))
 
 
 def pairs_of(size, step):
@@ -338,11 +358,14 @@
         after.append(lax.ppermute(gated[c], "ctx", down))
     product, pn, pr, tm, tb = prep(conv_filter, key_rows, value_rows)
     before = lax.ppermute(product, "ctx", up)
-    old = ()
-    for c in range(PARTS):
-        old = back(tb, pr, gated[c], after[c], key_rows, value_rows, c * width, old)
-    grad_key, grad_value, partial = old
+
+    def run(c, old, *kinds):
+        return back(tb, pr, gated[c], after[c], key_rows, value_rows, c * width, old, *kinds)
+
+    grad_key, grad_value, partial = run(0, ())
+    (partial,) = run(1, (partial,), True, False)
     own = reduce_filter(partial, size)
+    grad_key, grad_value = run(1, (grad_key, grad_value), False, True)
     (grad_query,) = mixed(tm, pn, before, grad_out)
     scale = 1.0 / math.sqrt(query_rows.shape[0] * size * GSIZE)
     return grad_query, grad_key, grad_value, own * scale

time: 55.4 us -> 56.8 us (1.025)
  Pallas kernels: 20.3 us -> 22.9 us
  waiting for transfers between devices: 6.1 us -> 4.85 us
    pallas_call x2 -> x3, Pallas kernels: 9.45 us -> 12 us  [back(): pl.pallas_call(lambda *refs: back_kernel(refs, sums_too, rows_too), out_s...]
    ppermute x4, waiting for transfers between devices: 6.1 us -> 4.84 us  [reduce_filter(): got = lax.ppermute(send, 'ctx', pairs_of(size, 1 << b))]
  transfers between devices with their start and end apart: 7 -> 7, of which waited for: 4 -> 3; matrix products, arithmetic and copies ran while one was open for 1% -> 1% of each run, Pallas kernels for 19% -> 25%
where the time goes in v6:
time: 56.8 us; the launch traced here: 56.4 us
  starting transfers between devices  25.3 us (45%)
  Pallas kernels  22.9 us (40%)
  waiting for transfers between devices  4.85 us (9%)
  other arithmetic  2.54 us (4%)
  between operations  0.75 us (1%)
    ppermute x4, starting transfers between devices, reduce_filter(): got = lax.ppermute(send, 'ctx', pairs_of(size, 1 << b))  20.9 us
    pallas_call x3, Pallas kernels, back(): pl.pallas_call(lambda *refs: back_kernel(refs, sums_too, rows_too), out_s...  12 us
    pallas_call x1, Pallas kernels, prep(): pl.pallas_call(prep_kernel, out_shape=(shape(*k.shape), r, r, t, t), grid...  5.71 us
    pallas_call x1, Pallas kernels, streamed(): pl.pallas_call(kernel, out_shape=tuple((x[0] for x in outs)), in_specs=[a...  5.17 us
    ppermute x4, waiting for transfers between devices, reduce_filter(): got = lax.ppermute(send, 'ctx', pairs_of(size, 1 << b))  4.84 us
    ppermute x2, starting transfers between devices, shards(): after.append(lax.ppermute(gated[c], 'ctx', down))  2.58 us
    convert_element_type x1, other arithmetic, shards(): (grad_out[:, cut].astype(f32) * query_rows[:, cut].astype(f32)).astype(bf)  1.91 us
    ppermute x1, starting transfers between devices, shards(): before = lax.ppermute(product, 'ctx', up)  1.83 us
  transfers between devices with their start and end apart: 7, of which 3 were waited for; matrix products, arithmetic and copies ran while one was open for 1% of the time, Pallas kernels for 25%

profile of v6, /device:TPU:0, one launch (start us, length us, event | category | flops | bytes accessed | tf_op | source)
XLA Modules:
  0.0 56.4 jit_solution(11644835537639335456)
XLA Ops:
  0.6 1.9 %multiply_convert_fusion = (bf16[128,2048]{1,0:T(8,128)(2,1)S(1)}, bf16[128,2048]{1,0:T(8,128)(2,1)S(1)}) fusion(bf16[128,4096]{1,0:T(8,128)(2,1)} %param.5, bf16[128,4096]{1,0:T(8,128)(2,1)} %refs_3_.2), kind=kLoop, calls=%fused_computation | loop fusion | flops 2097152 | bytes 3145728 | tf_op jit(solution)/shard_map/convert_element_type | solution.py:357
  2.5 0.0 copy-start.1
  2.6 0.0 copy-start
  2.6 1.3 %collective-permute-start.2 = (bf16[128,2048]{1,0:T(8,128)(2,1)S(1)}, bf16[128,2048]{1,0:T(8,128)(2,1)S(1)}, u32[]{:S(2)}, u32[]{:S(2)}) collective-permute-start(bf16[128,2048]{1,0:T(8,128)(2,1)S(1)} %get-tuple-element.24.refs_2_), channel_id=1, source_target_pairs={{1,0},{2,1},{3,2},{4,3},{5,4},{6,5},{7,6},{8,7},{9,8},{10,9},{11,1... | collective-permute-start | bytes 1572872 | tf_op jit(solution)/shard_map/ppermute | solution.py:358
  3.9 1.3 %collective-permute-start.1 = (bf16[128,2048]{1,0:T(8,128)(2,1)S(1)}, bf16[128,2048]{1,0:T(8,128)(2,1)S(1)}, u32[]{:S(2)}, u32[]{:S(2)}) collective-permute-start(bf16[128,2048]{1,0:T(8,128)(2,1)S(1)} %get-tuple-element.25.refs_1_), channel_id=1, source_target_pairs={{1,0},{2,1},{3,2},{4,3},{5,4},{6,5},{7,6},{8,7},{9,8},{10,9},{11,1... | collective-permute-start | bytes 1572872 | tf_op jit(solution)/shard_map/ppermute | solution.py:358
  5.2 5.7 %prep.1 = (bf16[128,4096]{1,0:T(8,128)(2,1)}, bf16[4096,128]{1,0:T(8,128)(2,1)}, bf16[4096,128]{1,0:T(8,128)(2,1)}, bf16[8192,128]{1,0:T(8,128)(2,1)}, bf16[8192,128]{1,0:T(8,128)(2,1)}) custom-call(bf16[256,128]{1,0:T(8,128)(2,1)} %h_ref.1, bf16[128,4096]{1,0:T(8,128)(2,1)} %refs_3_.3, bf16[128,4096]{1,0:T(8,128)(2,1)} %refs_4_.3), custom_call_target="tpu_custom_call" | custom-call | tf_op jit(solution)/shard_map/prep/pallas_call | solution.py:215
  10.9 0.0 collective-permute-done.2.refs_3_
  10.9 0.0 copy-done.1
  10.9 4.7 %back.3 = (bf16[128,4096]{1,0:T(8,128)(2,1)}, bf16[128,4096]{1,0:T(8,128)(2,1)}, f32[256,128]{1,0:T(8,128)S(1)}) custom-call(bf16[8192,128]{1,0:T(8,128)(2,1)} %get-tuple-element.17.refs_0_, bf16[4096,128]{1,0:T(8,128)(2,1)} %get-tuple-element.18.refs_1_.refs_0_, bf16[128,2048]{1,0:T(8,128)(2,1)} %copy-done.1, ...), custom_call_target="tpu_custom_call" | custom-call | tf_op jit(solution)/shard_map/back/pallas_call | solution.py:312
  15.6 0.0 copy-done
  15.6 0.0 copy-start.2
  15.6 0.0 collective-permute-done.1.refs_2_
  15.6 3.5 %back.5 = f32[256,128]{1,0:T(8,128)S(1)} custom-call(bf16[4096,128]{1,0:T(8,128)(2,1)} %get-tuple-element.18.refs_1_.refs_0_, bf16[128,2048]{1,0:T(8,128)(2,1)} %copy-done, bf16[128,2048]{1,0:T(8,128)(2,1)S(1)} %collective-permute-done.1.refs_2_, f32[256,128]{1,0:T(8,128)S(1)} %get-tuple-element.23.refs_3_), custom_call_target="tpu_custom_call", output_to_operand_aliasing={{}: (3, {})} | custom-call | tf_op jit(solution)/shard_map/back/pallas_call | solution.py:312
  19.2 5.8 %collective-permute-start.3 = (f32[2,2,2,16,128]{4,3,2,1,0:T(8,128)S(1)}, f32[2,2,2,16,128]{4,3,2,1,0:T(8,128)S(1)}, u32[]{:S(2)}, u32[]{:S(2)}) collective-permute-start(f32[2,2,2,16,128]{4,3,2,1,0:T(8,128)S(1)} %dynamic-slice_bitcast_fusion), channel_id=1, source_target_pairs={{0,4},{1,5},{2,6},{3,7},{4,0},{5,1},{6,2},{7,3},{8,12},{9,13},{10,... | collective-permute-start | bytes 196616 | tf_op jit(solution)/shard_map/ppermute | solution.py:339
  25.0 0.0 copy-done.2
  25.0 1.8 %collective-permute-start = (bf16[128,4096]{1,0:T(8,128)(2,1)S(1)}, bf16[128,4096]{1,0:T(8,128)(2,1)S(1)}, u32[]{:S(2)}, u32[]{:S(2)}) collective-permute-start(bf16[128,4096]{1,0:T(8,128)(2,1)S(1)} %copy-done.2), channel_id=1, source_target_pairs={{0,1},{1,2},{2,3},{3,4},{4,5},{5,6},{6,7},{7,8},{8,9},{9,10},{10,1... | collective-permute-start | bytes 3145736 | tf_op jit(solution)/shard_map/ppermute | solution.py:360
  26.8 0.7 %collective-permute-done.3 = f32[2,2,2,16,128]{4,3,2,1,0:T(8,128)S(1)} collective-permute-done((f32[2,2,2,16,128]{4,3,2,1,0:T(8,128)S(1)}, f32[2,2,2,16,128]{4,3,2,1,0:T(8,128)S(1)}, u32[]{:S(2)}, u32[]{:S(2)}) %collective-permute-start.3) | collective-permute-done | bytes 65568 | tf_op jit(solution)/shard_map/ppermute | solution.py:339
  27.6 1.6 %collective-permute-start.4 = (f32[2,2,16,128]{3,2,1,0:T(8,128)S(1)}, f32[2,2,16,128]{3,2,1,0:T(8,128)S(1)}, u32[]{:S(2)}, u32[]{:S(2)}) collective-permute-start(f32[2,2,16,128]{3,2,1,0:T(8,128)S(1)} %dynamic-slice_bitcast_fusion.1), channel_id=1, source_target_pairs={{0,2},{1,3},{2,0},{3,1},{4,6},{5,7},{6,4},{7,5},{8,10},{9,11},{10,... | collective-permute-start | bytes 98312 | tf_op jit(solution)/shard_map/ppermute | solution.py:339
  29.2 2.3 %collective-permute-done.4 = f32[2,2,16,128]{3,2,1,0:T(8,128)S(1)} collective-permute-done((f32[2,2,16,128]{3,2,1,0:T(8,128)S(1)}, f32[2,2,16,128]{3,2,1,0:T(8,128)S(1)}, u32[]{:S(2)}, u32[]{:S(2)}) %collective-permute-start.4) | collective-permute-done | bytes 32800 | tf_op jit(solution)/shard_map/ppermute | solution.py:339
  31.6 13.4 %collective-permute-start.5 = (f32[2,16,128]{2,1,0:T(8,128)S(1)}, f32[2,16,128]{2,1,0:T(8,128)S(1)}, u32[]{:S(2)}, u32[]{:S(2)}) collective-permute-start(f32[2,16,128]{2,1,0:T(8,128)S(1)} %dynamic-slice_bitcast_fusion.2), channel_id=1, source_target_pairs={{0,8},{1,9},{2,10},{3,11},{4,12},{5,13},{6,14},{7,15},{8,0},{9,1},... | collective-permute-start | bytes 49160 | tf_op jit(solution)/shard_map/ppermute | solution.py:339
  45.0 1.8 %collective-permute-done.5 = f32[2,16,128]{2,1,0:T(8,128)S(1)} collective-permute-done((f32[2,16,128]{2,1,0:T(8,128)S(1)}, f32[2,16,128]{2,1,0:T(8,128)S(1)}, u32[]{:S(2)}, u32[]{:S(2)}) %collective-permute-start.5) | collective-permute-done | bytes 16416 | tf_op jit(solution)/shard_map/ppermute | solution.py:339
  46.8 0.0 collective-permute-start.6
  46.8 3.8 %back.4 = (bf16[128,4096]{1,0:T(8,128)(2,1)}, bf16[128,4096]{1,0:T(8,128)(2,1)}) custom-call(bf16[8192,128]{1,0:T(8,128)(2,1)} %get-tuple-element.17.refs_0_, bf16[128,2048]{1,0:T(8,128)(2,1)} %copy-done, bf16[128,2048]{1,0:T(8,128)(2,1)S(1)} %collective-permute-done.1.refs_2_, ...), custom_call_target="tpu_custom_call", output_to_operand_aliasing={{0}: (5, {}), {1}: (6, {})} | custom-call | tf_op jit(solution)/shard_map/back/pallas_call | solution.py:312
  50.7 0.0 collective-permute-done.6
  50.7 0.6 %fusion = f32[16,128]{1,0:T(8,128)} fusion(f32[16,128]{1,0:T(8,128)S(1)} %collective-permute-done.6, f32[2,16,128]{2,1,0:T(8,128)S(1)} %bitcast_add_fusion.2, s32[]{:T(128)S(6)} %select_n.34), kind=kLoop, calls=%fused_computation.9 | loop fusion | flops 4096 | bytes 24580 | tf_op jit(solution)/shard_map/mul | solution.py:371
  51.3 0.0 collective-permute-done.refs_2_
  51.3 5.2 %shard_map.84 = bf16[128,4096]{1,0:T(8,128)(2,1)} custom-call(bf16[8192,128]{1,0:T(8,128)(2,1)} %get-tuple-element.14.refs_0_, bf16[4096,128]{1,0:T(8,128)(2,1)} %get-tuple-element.15.refs_1_, bf16[128,4096]{1,0:T(8,128)(2,1)S(1)} %collective-permute-done.refs_2_, bf16[128,4096]{1,0:T(8,128)(2,1)} %refs_3_.2), custom_call_target="tpu_custom_call" | custom-call | tf_op jit(solution)/shard_map/pallas_call | solution.py:277
  (7 shorter events, 0.1 us)
Async XLA Ops:
  2.5 8.3 %copy-start.1 = (bf16[128,2048]{1,0:T(8,128)(2,1)}, bf16[128,2048]{1,0:T(8,128)(2,1)S(1)}, u32[]{:S(2)}) copy-start(bf16[128,2048]{1,0:T(8,128)(2,1)S(1)} %get-tuple-element.24.refs_2_) | copy-start | bytes 1572868
  2.6 13.0 %copy-start = (bf16[128,2048]{1,0:T(8,128)(2,1)}, bf16[128,2048]{1,0:T(8,128)(2,1)S(1)}, u32[]{:S(2)}) copy-start(bf16[128,2048]{1,0:T(8,128)(2,1)S(1)} %get-tuple-element.25.refs_1_) | copy-start | bytes 1572868
  2.6 8.3 %collective-permute-start.2 = (bf16[128,2048]{1,0:T(8,128)(2,1)S(1)}, bf16[128,2048]{1,0:T(8,128)(2,1)S(1)}, u32[]{:S(2)}, u32[]{:S(2)}) collective-permute-start(bf16[128,2048]{1,0:T(8,128)(2,1)S(1)} %get-tuple-element.24.refs_2_), channel_id=1, source_target_pairs={{1,0},{2,1},{3,2},{4,3},{5,4},{6,5},{7,6},{8,7},{9,8},{10,9},{11,1... | collective-permute-start | bytes 1572872 | tf_op jit(solution)/shard_map/ppermute | solution.py:358
  3.9 11.7 %collective-permute-start.1 = (bf16[128,2048]{1,0:T(8,128)(2,1)S(1)}, bf16[128,2048]{1,0:T(8,128)(2,1)S(1)}, u32[]{:S(2)}, u32[]{:S(2)}) collective-permute-start(bf16[128,2048]{1,0:T(8,128)(2,1)S(1)} %get-tuple-element.25.refs_1_), channel_id=1, source_target_pairs={{1,0},{2,1},{3,2},{4,3},{5,4},{6,5},{7,6},{8,7},{9,8},{10,9},{11,1... | collective-permute-start | bytes 1572872 | tf_op jit(solution)/shard_map/ppermute | solution.py:358
  15.6 9.4 %copy-start.2 = (bf16[128,4096]{1,0:T(8,128)(2,1)S(1)}, bf16[128,4096]{1,0:T(8,128)(2,1)}, u32[]{:S(2)}) copy-start(bf16[128,4096]{1,0:T(8,128)(2,1)} %get-tuple-element.16) | copy-start | bytes 3145732
  19.2 8.4 %collective-permute-start.3 = (f32[2,2,2,16,128]{4,3,2,1,0:T(8,128)S(1)}, f32[2,2,2,16,128]{4,3,2,1,0:T(8,128)S(1)}, u32[]{:S(2)}, u32[]{:S(2)}) collective-permute-start(f32[2,2,2,16,128]{4,3,2,1,0:T(8,128)S(1)} %dynamic-slice_bitcast_fusion), channel_id=1, source_target_pairs={{0,4},{1,5},{2,6},{3,7},{4,0},{5,1},{6,2},{7,3},{8,12},{9,13},{10,... | collective-permute-start | bytes 196616 | tf_op jit(solution)/shard_map/ppermute | solution.py:339
  25.0 26.3 %collective-permute-start = (bf16[128,4096]{1,0:T(8,128)(2,1)S(1)}, bf16[128,4096]{1,0:T(8,128)(2,1)S(1)}, u32[]{:S(2)}, u32[]{:S(2)}) collective-permute-start(bf16[128,4096]{1,0:T(8,128)(2,1)S(1)} %copy-done.2), channel_id=1, source_target_pairs={{0,1},{1,2},{2,3},{3,4},{4,5},{5,6},{6,7},{7,8},{8,9},{9,10},{10,1... | collective-permute-start | bytes 3145736 | tf_op jit(solution)/shard_map/ppermute | solution.py:360
  27.6 4.0 %collective-permute-start.4 = (f32[2,2,16,128]{3,2,1,0:T(8,128)S(1)}, f32[2,2,16,128]{3,2,1,0:T(8,128)S(1)}, u32[]{:S(2)}, u32[]{:S(2)}) collective-permute-start(f32[2,2,16,128]{3,2,1,0:T(8,128)S(1)} %dynamic-slice_bitcast_fusion.1), channel_id=1, source_target_pairs={{0,2},{1,3},{2,0},{3,1},{4,6},{5,7},{6,4},{7,5},{8,10},{9,11},{10,... | collective-permute-start | bytes 98312 | tf_op jit(solution)/shard_map/ppermute | solution.py:339
  31.6 15.2 %collective-permute-start.5 = (f32[2,16,128]{2,1,0:T(8,128)S(1)}, f32[2,16,128]{2,1,0:T(8,128)S(1)}, u32[]{:S(2)}, u32[]{:S(2)}) collective-permute-start(f32[2,16,128]{2,1,0:T(8,128)S(1)} %dynamic-slice_bitcast_fusion.2), channel_id=1, source_target_pairs={{0,8},{1,9},{2,10},{3,11},{4,12},{5,13},{6,14},{7,15},{8,0},{9,1},... | collective-permute-start | bytes 49160 | tf_op jit(solution)/shard_map/ppermute | solution.py:339
  46.8 3.8 %collective-permute-start.6 = (f32[16,128]{1,0:T(8,128)S(1)}, f32[16,128]{1,0:T(8,128)S(1)}, u32[]{:S(2)}, u32[]{:S(2)}) collective-permute-start(f32[16,128]{1,0:T(8,128)S(1)} %dynamic-slice_bitcast_fusion.3), channel_id=1, source_target_pairs={{0,1},{1,0},{2,3},{3,2},{4,5},{5,4},{6,7},{7,6},{8,9},{9,8},{10,11... | collective-permute-start | bytes 24584 | tf_op jit(solution)/shard_map/ppermute | solution.py:339
